TPU v7x, 256 devices: a whole 4x4x8 slice. The times are simulated.
256 devices in a mesh: row: 16 (over x, y_hi, core), col: 16 (over z, y_lo).
Axes of the slice: x: 4, y: 4 (y_hi: 2, y_lo: 2; y = y_hi * 2 + y_lo), z: 8, core: 2. Of those that a mesh axis runs over, the one named last changes fastest.
Arguments:
- positions: float32 [3, 16384], P(None, ('row', 'col')), may hold values from -0.2 to 63.2, as said below
- radii: float32 [16384], P(('row', 'col')), may hold values from 0.1 to 0.28
- basis: float32 [32, 3, 16384], P(None, None, ('row', 'col')), may hold values from -0.0112763724 to 0.0112763724, as said below
- rhs: float32 [3, 16384], P(None, ('row', 'col')), may hold values from -6 to 6
Outputs:
- solution: float32 [3, 16384], P(None, ('row', 'col'))
- residual: float32 [3, 16384], P(None, ('row', 'col'))
Inputs may be any that keep to these rules, and one draw needn't show every extreme that they name: `positions`: every coordinate lies within 0.2 of a whole number and any two centres are 0.6 or more apart, more than the sum of any two radii. `basis`: the 32 vectors are linearly independent.
All inputs are finite; a program needn't handle non-finite values.
Results may differ from a plain program's by a relative error of at most 0.0003.
Values sent between devices are 32-bit elements; how exact they have to be, the bound alone decides.
A program may use at most 64 MiB of HBM per device.

v0:
```python
import math

import jax
import jax.numpy as jnp
from jax import lax
from jax.sharding import PartitionSpec as P

ITERS = 2


far_scale = 1.0 / (8.0 * math.pi)
self_scale = 1.0 / (6.0 * math.pi)
highest = lax.Precision.HIGHEST


def contract(left, right):
    return lax.dot_general(
        left, right, (((1,), (1,)), ((), ())), precision=highest, preferred_element_type=jnp.float32
    )


def block_apply(out_pos, out_rad, out_index, in_pos, in_rad, in_index, fields):
    deltas = [out_pos[axis_id][:, None] - in_pos[axis_id][None, :] for axis_id in range(3)]
    coincide = out_index[:, None] == in_index[None, :]
    dist_sq = deltas[0] * deltas[0] + deltas[1] * deltas[1] + deltas[2] * deltas[2]
    safe_sq = jnp.where(coincide, jnp.ones_like(dist_sq), dist_sq)
    inv_sq = 1.0 / safe_sq
    inv_dist = jnp.sqrt(inv_sq)
    radius_sum = (out_rad * out_rad)[:, None] + (in_rad * in_rad)[None, :]
    scaled = far_scale * inv_dist
    isotropic = scaled * (1.0 + radius_sum * inv_sq / 3.0)
    own_term = jnp.broadcast_to((self_scale / out_rad)[:, None], isotropic.shape)
    isotropic = jnp.where(coincide, own_term, isotropic)
    along = jnp.where(
        coincide, jnp.zeros_like(dist_sq), scaled * (1.0 - radius_sum * inv_sq) * inv_sq
    )
    tensors = {}
    for first in range(3):
        for second in range(first, 3):
            entry = along * deltas[first] * deltas[second]
            if first == second:
                entry = entry + isotropic
            tensors[first, second] = entry
    results = []
    for first in range(3):
        total = None
        for second in range(3):
            term = contract(fields[:, second, :], tensors[min(first, second), max(first, second)])
            total = term if total is None else total + term
        results.append(total)
    return jnp.stack(results, axis=1)


def field_apply(out_pos, out_rad, out_index, in_pos, in_rad, in_index, fields, width):
    count = out_rad.shape[0] // width
    pos_blocks = out_pos.reshape(3, count, width).transpose(1, 0, 2)
    rad_blocks = out_rad.reshape(count, width)
    index_blocks = out_index.reshape(count, width)

    def one_block(packed):
        return block_apply(packed[0], packed[1], packed[2], in_pos, in_rad, in_index, fields)

    stacked = lax.map(one_block, (pos_blocks, rad_blocks, index_blocks))
    return stacked.transpose(1, 2, 0, 3).reshape(fields.shape[0], 3, count * width)


def body(positions, radii, basis, rhs):
    cols_count = lax.axis_size("col")
    row_id = lax.axis_index("row")
    col_id = lax.axis_index("col")
    width = positions.shape[1]
    vectors_count = basis.shape[0]
    target_pos, target_rad = (
        lax.all_gather(positions, "row", axis=1, tiled=True),
        lax.all_gather(radii, "row", axis=0, tiled=True),
    )
    source_pos, source_rad = (
        lax.all_gather(positions, "col", axis=1, tiled=True),
        lax.all_gather(radii, "col", axis=0, tiled=True),
    )
    target_span = target_rad.shape[0]
    source_span = source_rad.shape[0]
    target_order = jnp.arange(target_span, dtype=jnp.int32)
    target_index = (target_order // width * cols_count + col_id) * width + target_order % width
    source_index = row_id * (cols_count * width) + jnp.arange(source_span, dtype=jnp.int32)

    def fold_sources(carry, piece):
        count = piece.shape[2]
        in_pos = lax.slice_in_dim(source_pos, 0, count, axis=1)
        in_rad = lax.slice_in_dim(source_rad, 0, count, axis=0)
        in_index = lax.slice_in_dim(source_index, 0, count, axis=0)
        return carry + field_apply(
            target_pos, target_rad, target_index, in_pos, in_rad, in_index, piece, width
        )

    empty_rows = jnp.zeros((vectors_count, 3, target_span), jnp.float32)
    partial_basis = fold_sources(
        empty_rows, jax.tree.map(lambda a: lax.all_gather(a, "col", axis=2, tiled=True), basis)
    )
    basis_image = lax.psum_scatter(partial_basis, "row", scatter_dimension=2, tiled=True)
    gram_part = jnp.einsum("kcp,lcp->kl", basis, basis_image, precision=highest)
    load_part = jnp.einsum("kcp,cp->k", basis, rhs, precision=highest)
    gram, load = lax.psum((gram_part, load_part), ("row", "col"))
    factor = jnp.linalg.cholesky(gram)

    def coarse_solve(vector):
        return jax.scipy.linalg.cho_solve((factor, True), vector)

    def combine(weights, fields):
        return jnp.einsum("k,kcp->cp", weights, fields, precision=highest)

    def correlation_of(field):
        return jnp.einsum("kcp,cp->k", basis_image, field, precision=highest)

    coarse = coarse_solve(load)
    solution = combine(coarse, basis)
    residual = rhs - combine(coarse, basis_image)

    def residual_stats(field):
        return lax.psum((correlation_of(field), jnp.sum(field * field)), ("row", "col"))

    correlation, norm_now = residual_stats(residual)
    projection = coarse_solve(correlation)
    direction = residual - combine(projection, basis)
    for iteration in range(ITERS):
        empty = jnp.zeros((1, 3, target_span), jnp.float32)
        partial_image = fold_sources(
            empty,
            jax.tree.map(lambda a: lax.all_gather(a, "col", axis=2, tiled=True), direction[None]),
        )
        image = lax.psum_scatter(partial_image, "row", scatter_dimension=2, tiled=True)[0]
        curvature = lax.psum(jnp.sum(direction * image), ("row", "col"))
        step_size = norm_now / curvature
        solution = solution + step_size * direction
        residual = residual - step_size * image
        if iteration + 1 < ITERS:
            correlation, norm_next = residual_stats(residual)
            projection = coarse_solve(correlation)
            direction = residual + norm_next / norm_now * direction - combine(projection, basis)
            norm_now = norm_next
    return (solution, residual)


def solution(mesh):
    return jax.shard_map(
        body,
        mesh=mesh,
        in_specs=(
            P(None, ("row", "col")),
            P(("row", "col")),
            P(None, None, ("row", "col")),
            P(None, ("row", "col")),
        ),
        out_specs=(P(None, ("row", "col")), P(None, ("row", "col"))),
        check_vma=False,
    )
```

profile of v0, /device:TPU:1, one launch (start us, length us, event | category | flops | bytes accessed | tf_op | source)
XLA Modules:
  0.0 1161.8 jit_solution(4575639744863065165)
XLA Ops:
  7.2 26.0 %all-gather.2 = f32[16,64,3]{1,2,0:T(4,128)S(1)} all-gather(f32[1,64,3]{1,2,0:T(4,128)} %bitcast.659), channel_id=1, replica_groups=mesh['row'=16,'col'=16] {'row'}, dimensions={0}, use_global_device_ids=true | all-gather | bytes 13056 | tf_op jit(solution)/shard_map/all_gather | solution.py:74
  33.2 28.7 %all-gather.3 = f32[16,64,3]{1,2,0:T(4,128)S(1)} all-gather(f32[1,64,3]{1,2,0:T(4,128)} %bitcast.660), channel_id=1, replica_groups=mesh['row'=16,'col'=16] {'col'}, dimensions={0}, use_global_device_ids=true | all-gather | bytes 13056 | tf_op jit(solution)/shard_map/all_gather | solution.py:78
  61.8 1.3 dynamic-slice
  63.8 0.9 dynamic-update-slice.3
  64.6 39.9 %all-reduce = f32[1024]{0:T(1024)S(1)} all-reduce(f32[1024]{0:T(1024)S(1)} %dynamic-update-slice.3), channel_id=1, replica_groups=mesh['row'=16,'col'=16] {'row'}, use_global_device_ids=true, to_apply=%add | all-reduce | flops 1024 | bytes 8192
  104.6 1.3 dynamic-slice.1
  106.5 0.9 dynamic-update-slice.4
  107.4 23.7 %all-reduce.1 = f32[1024]{0:T(1024)S(1)} all-reduce(f32[1024]{0:T(1024)S(1)} %dynamic-update-slice.4), channel_id=1, replica_groups=mesh['row'=16,'col'=16] {'col'}, use_global_device_ids=true, to_apply=%add.1 | all-reduce | flops 1024 | bytes 8192
  131.4 0.9 copy.39
  132.3 49.4 %all_gather.25 = f32[32,3,1024]{0,1,2:T(4,128)S(1)} all-gather(f32[32,3,64]{0,1,2:T(4,128)S(1)} %copy.39), channel_id=1, replica_groups=mesh['row'=16,'col'=16] {'col'}, dimensions={2}, use_global_device_ids=true | all-gather | bytes 417792 | tf_op jit(solution)/shard_map/all_gather | solution.py:98
  182.6 103.6 %while.39 = (s32[]{:T(128)}, f32[16,32,3,64]{3,1,2,0:T(8,128)S(1)}, s32[16,64]{1,0:T(8,128)S(1)}, f32[16,3,64]{2,1,0:T(4,128)S(1)}, f32[3,1024]{1,0:T(4,128)S(1)...) while((s32[]{:T(128)}, f32[16,32,3,64]{3,1,2,0:T(8,128)S(1)}, ...), condition=%wide.region_1.2_spmd.clone, body=%wide.region_0.1_spmd.clone.sunk | while | flops 239297664 | bytes 2417017 | solution.py:63
  286.2 0.9 copy.64
  287.2 1.5 reshape.352
  288.9 75.8 %reduce-scatter.10.cloned.1.call-done = f32[64,96]{1,0:T(8,128)} async-done(((f32[1024,96]{1,0:T(8,128)}), f32[64,96]{1,0:T(8,128)}) %reduce-scatter.10.cloned.1.call-update) | async-done | bytes 24592
  364.8 0.9 reshape.353
  366.0 77.7 %all-reduce.4 = (f32[32,32]{0,1:T(8,128)S(1)}, f32[32]{0:T(128)S(1)}) all-reduce(f32[32,32]{0,1:T(8,128)S(1)} %convolution_bitcast_fusion.18, f32[32]{0:T(128)S(1)} %convolution_bitcast_fusion.27), channel_id=1, replica_groups=mesh['row'=16,'col'=16] {'row','col'}, use_global_device_ids=true, to_apply=%region_3.4 | all-reduce | flops 1056 | bytes 8448 | tf_op jit(solution)/shard_map/psum | solution.py:103
  443.7 2.9 cholesky.18
  447.9 2.4 custom-call.10
  451.6 73.1 %psum.59 = f32[32]{0:T(128)S(1)} all-reduce(f32[32]{0:T(128)S(1)} %convolution_bitcast_fusion.26), channel_id=1, replica_groups=mesh['row'=16,'col'=16] {'row','col'}, use_global_device_ids=true, to_apply=%region_9.11 | all-reduce | flops 32 | bytes 256 | tf_op jit(solution)/shard_map/psum | solution.py:120
  525.1 24.3 %all-gather.4 = f32[16,64,3]{1,2,0:T(4,128)S(1)} all-gather(f32[1,64,3]{1,2,0:T(4,128)S(1)} %bitcast.652), channel_id=2, replica_groups=mesh['row'=16,'col'=16] {'col'}, dimensions={0}, use_global_device_ids=true | all-gather | bytes 13056 | tf_op jit(solution)/shard_map/all_gather | solution.py:129
  549.6 95.1 %while.40 = (s32[]{:T(128)}, f32[16,1,3,64]{3,2,1,0:T(4,128)S(1)}, s32[16,64]{1,0:T(8,128)S(1)}, f32[16,3,64]{2,1,0:T(4,128)S(1)}, f32[3,1024]{1,0:T(4,128)S(1)}...) while((s32[]{:T(128)}, f32[16,1,3,64]{3,2,1,0:T(4,128)S(1)}, ...), condition=%wide.region_11.13_spmd.clone, body=%wide.region_10.12_spmd.clone.sunk | while | flops 19859328 | bytes 287865 | solution.py:63
  644.7 0.9 copy.60
  645.6 1.9 bitcast_reduce_fusion
  647.7 74.9 %reduce-scatter.12.cloned.1.call-done = f32[64,3]{1,0:T(8,128)} async-done(((f32[1024,3]{1,0:T(8,128)}), f32[64,3]{1,0:T(8,128)}) %reduce-scatter.12.cloned.1.call-update) | async-done | bytes 784
  722.5 0.9 reshape_bitcast_fusion
  724.2 77.5 %all-reduce.3 = (f32[]{:T(128)}, f32[]{:T(128)}) all-reduce(f32[]{:T(128)} %get-tuple-element.527, f32[]{:T(128)} %fusion.251), channel_id=1, replica_groups=mesh['row'=16,'col'=16] {'row','col'}, use_global_device_ids=true, to_apply=%region_8.10 | all-reduce | flops 2 | bytes 16 | tf_op jit(solution)/shard_map/psum | solution.py:120
  804.0 73.6 %all-reduce.2 = (f32[32]{0:T(128)S(1)}, f32[]{:T(128)}) all-reduce(f32[32]{0:T(128)S(1)} %convolution_bitcast_fusion.25, f32[]{:T(128)} %get-tuple-element.525), channel_id=1, replica_groups=mesh['row'=16,'col'=16] {'row','col'}, use_global_device_ids=true, to_apply=%region_17.19 | all-reduce | flops 33 | bytes 264 | tf_op jit(solution)/shard_map/psum | solution.py:120
  879.3 23.9 %all-gather.5 = f32[16,64,3]{1,2,0:T(4,128)S(1)} all-gather(f32[1,64,3]{1,2,0:T(4,128)S(1)} %bitcast.654), channel_id=3, replica_groups=mesh['row'=16,'col'=16] {'col'}, dimensions={0}, use_global_device_ids=true | all-gather | bytes 13056 | tf_op jit(solution)/shard_map/all_gather | solution.py:129
  903.2 95.1 %while.41 = (s32[]{:T(128)}, f32[16,1,3,64]{3,2,1,0:T(4,128)S(1)}, s32[16,64]{1,0:T(8,128)S(1)}, f32[16,3,64]{2,1,0:T(4,128)S(1)}, f32[3,1024]{1,0:T(4,128)S(1)}...) while((s32[]{:T(128)}, f32[16,1,3,64]{3,2,1,0:T(4,128)S(1)}, ...), condition=%wide.region_19.21_spmd.clone, body=%wide.region_18.20_spmd.clone.sunk | while | flops 19859328 | bytes 287865 | solution.py:63
  998.3 1.0 copy.65
  999.4 74.9 %reduce-scatter.14.cloned.1.call-done = f32[64,3]{1,0:T(8,128)} async-done(((f32[1024,3]{1,0:T(8,128)}), f32[64,3]{1,0:T(8,128)}) %reduce-scatter.14.cloned.1.call-update) | async-done | bytes 784
  1075.9 77.5 %psum.63 = f32[]{:T(128)} all-reduce(f32[]{:T(128)} %fusion.253), channel_id=1, replica_groups=mesh['row'=16,'col'=16] {'row','col'}, use_global_device_ids=true, to_apply=%region_22.24 | all-reduce | flops 1 | bytes 8 | tf_op jit(solution)/shard_map/psum | solution.py:132
  (844 shorter events, 297.2 us)
Async XLA Ops:
  7.2 357.6 %reduce-scatter.10.cloned.1.call-start = ((), (), s32[]{:S(2)}) async-start(), calls=%async_computation.3 | async-start | bytes 557056
  287.2 1.6 copy-start
  287.2 1.6 copy-start.1
  288.7 433.8 %reduce-scatter.12.cloned.1.call-start = ((), (), s32[]{:S(2)}) async-start(), calls=%async_computation.4 | async-start | bytes 557056
  647.6 426.7 %reduce-scatter.14.cloned.1.call-start = ((), (), s32[]{:S(2)}) async-start(), calls=%async_computation.5 | async-start | bytes 557056
Sparse Core Ops, SparseCore 0:
  288.9 75.8 reduce-scatter.9
  647.7 74.7 reduce-scatter.11
  999.5 74.7 reduce-scatter.13
where the time goes:
time: 1160 us
  blocking collectives  595 us (51%)
  matrix products  281 us (24%)
  waiting for transfers between devices  226 us (19%)
  local copies, waits for them, and re-layouts  21.8 us (2%)
  between operations  19.2 us (2%)
  other arithmetic  13.2 us (1%)
    dot_general x432, matrix products, contract(): lax.dot_general(left, right, (((1,), (1,)), ((), ())), precision=highest,...  278 us
    unnamed x6, waiting for transfers between devices  226 us
    psum x3, blocking collectives, residual_stats(): lax.psum((correlation_of(field), jnp.sum(field * field)), ('row', 'col'))  224 us
    all_gather x3, blocking collectives, body(): lax.all_gather(a, 'col', axis=2, tiled=True)  97.6 us
    psum x1, blocking collectives, body(): gram, load = lax.psum((gram_part, load_part), ('row', 'col'))  77.7 us
    psum x1, blocking collectives, body(): curvature = lax.psum(jnp.sum(direction * image), ('row', 'col'))  77.5 us
    unnamed x2, blocking collectives  63.6 us
    all_gather x1, blocking collectives, body(): lax.all_gather(positions, 'col', axis=1, tiled=True)  28.7 us
  transfers between devices with their start and end apart: 3, of which 3 were waited for; matrix products, arithmetic and copies ran while one was open for 0% of the time, Pallas kernels for 0%

commit v1 on v0

v1 whole, which is shorter than its diff:
```python
import functools
import math

import jax
import jax.numpy as jnp
from jax import lax
from jax.experimental import pallas as pl
from jax.experimental.pallas import tpu as pltpu
from jax.sharding import PartitionSpec as P

MESH = pl.DeviceIdType.MESH
F32 = jnp.float32
BF16 = jnp.bfloat16

far_scale = 1.0 / (8.0 * math.pi)
self_scale = 1.0 / (6.0 * math.pi)

LANES = 128
HALF = 64
PAIRS = ((0, 0), (1, 1), (2, 2), (0, 1), (1, 2), (2, 0))
SLOT = {}
for _slot, (_a, _b) in enumerate(PAIRS):
    SLOT[_a, _b] = _slot
    SLOT[_b, _a] = _slot


def kernel(
    n, vectors,
    geo_ref, wp_ref,
    sol_ref, res_ref,
    grow, gcol, wcol, src_b, tgt, mob, fields, aw_send, aw_recv, aw,
    gram_a, gram_row, gram_b, gram_col,
    vec_a, vec_col_a, stat_a, stat_row_a, part_a, part_row_a, stat_b, stat_col_b,
    vec_c, vec_col_c, stat_c, stat_row_c, part_c, part_row_c, stat_d, stat_col_d,
    stat_e, stat_row_e, stat_f, stat_col_f,
    send_sems, recv_sems,
):
    r = lax.axis_index("row")
    c = lax.axis_index("col")
    kh = vectors // 2
    span = n * HALF
    tiles = span // LANES

    lane1 = lax.broadcasted_iota(jnp.int32, (1, LANES), 1)
    lane8 = lax.broadcasted_iota(jnp.int32, (8, LANES), 1)
    lane_k = lax.broadcasted_iota(jnp.int32, (kh, LANES), 1)
    row_k = lax.broadcasted_iota(jnp.int32, (kh, LANES), 0)
    low1, low8, low_k = lane1 < HALF, lane8 < HALF, lane_k < HALF

    def swap(x):
        return pltpu.roll(x, HALF, 1)

    def to_row(src, dst, tag):
        def one(step, carry):
            peer = lax.rem(r + step, n)
            pltpu.make_async_remote_copy(
                src_ref=src(peer), dst_ref=dst.at[r], send_sem=send_sems.at[tag],
                recv_sem=recv_sems.at[tag], device_id=(peer, c), device_id_type=MESH,
            ).start()
            return carry
        lax.fori_loop(1, n, one, 0)

    def to_col(src, dst, tag):
        def one(step, carry):
            peer = lax.rem(c + step, n)
            pltpu.make_async_remote_copy(
                src_ref=src, dst_ref=dst.at[c], send_sem=send_sems.at[tag],
                recv_sem=recv_sems.at[tag], device_id=(r, peer), device_id_type=MESH,
            ).start()
            return carry
        lax.fori_loop(1, n, one, 0)

    def arrived(dst, tag):
        all_but_one = dst.at[pl.ds(0, n - 1)]
        pltpu.make_async_copy(all_but_one, all_but_one, recv_sems.at[tag]).wait()

    def departed(dst, tag):
        all_but_one = dst.at[pl.ds(0, n - 1)]
        pltpu.make_async_copy(all_but_one, all_but_one, send_sems.at[tag]).wait()

    def total(ref):
        parts = [ref[i] for i in range(n)]
        while len(parts) > 1:
            parts = [parts[i] + parts[i + 1] for i in range(0, len(parts), 2)]
        return parts[0]

    barrier = pltpu.get_barrier_semaphore()

    def greet(step, carry):
        pl.semaphore_signal(barrier, inc=1, device_id=(lax.rem(r + step, n), c), device_id_type=MESH)
        pl.semaphore_signal(barrier, inc=1, device_id=(r, lax.rem(c + step, n)), device_id_type=MESH)
        return carry
    lax.fori_loop(1, n, greet, 0)
    pl.semaphore_wait(barrier, 2 * (n - 1))

    to_col(geo_ref, gcol, 0)
    to_row(lambda peer: geo_ref, grow, 1)
    to_col(wp_ref, wcol, 2)
    gcol[c] = geo_ref[...]
    grow[r] = geo_ref[...]
    wcol[c] = wp_ref[...]

    def spread(ref, count):
        for p in range(tiles):
            tile = jnp.where(low8, ref[2 * p], ref[2 * p + 1])
            turned = tile.T
            for axis in range(count):
                src_b[axis, pl.ds(p * LANES, LANES), :] = jnp.broadcast_to(
                    turned[:, axis:axis + 1], (LANES, LANES)
                )

    arrived(gcol, 0)
    spread(gcol, 4)
    arrived(grow, 1)
    for q in range(tiles):
        tgt[:, q * LANES:(q + 1) * LANES] = jnp.where(low8, grow[2 * q], grow[2 * q + 1])

    def form_tile(q, carry):
        lanes = pl.ds(pl.multiple_of(q * LANES, LANES), LANES)
        tx, ty, tz, t_rad = [
            jnp.broadcast_to(tgt[axis:axis + 1, lanes], (8, LANES)) for axis in range(4)
        ]
        t_rad_sq = t_rad * t_rad
        own = self_scale / t_rad
        t_rel = lane8 + (q * LANES - r * HALF)
        t_key = jnp.where(jnp.logical_and(t_rel >= 0, t_rel < HALF), t_rel, -span)
        s_rel0 = lax.broadcasted_iota(jnp.int32, (8, LANES), 0) - c * HALF

        def form_row(i, inner):
            rows = pl.ds(pl.multiple_of(i * 8, 8), 8)
            sx, sy, sz, s_rad = [src_b[axis, rows, :] for axis in range(4)]
            s_rel = s_rel0 + i * 8
            same = s_rel == t_key
            dx, dy, dz = tx - sx, ty - sy, tz - sz
            dist_sq = dx * dx + dy * dy + dz * dz
            inv = lax.rsqrt(jnp.where(same, 1.0, dist_sq))
            inv_sq = inv * inv
            ratio = (t_rad_sq + s_rad * s_rad) * inv_sq
            scaled = far_scale * inv
            iso = jnp.where(same, own, scaled + scaled * (ratio * (1.0 / 3.0)))
            along = (scaled - scaled * ratio) * inv_sq
            ax, ay, az = along * dx, along * dy, along * dz
            mob[0, rows, lanes] = ax * dx + iso
            mob[1, rows, lanes] = ay * dy + iso
            mob[2, rows, lanes] = az * dz + iso
            mob[3, rows, lanes] = ax * dy
            mob[4, rows, lanes] = ay * dz
            mob[5, rows, lanes] = az * dx
            return inner
        lax.fori_loop(0, span // 8, form_row, 0, unroll=4)
        return carry
    lax.fori_loop(0, tiles, form_tile, 0)

    arrived(wcol, 2)
    for p in range(tiles):
        cols = slice(p * LANES, (p + 1) * LANES)
        for axis in range(3):
            first = wcol[2 * p, kh * axis:kh * (axis + 1), :]
            second = wcol[2 * p + 1, kh * axis:kh * (axis + 1), :]
            block = jnp.concatenate(
                [jnp.where(low_k, first, swap(second)), jnp.where(low_k, swap(first), second)], axis=0
            )
            high = block.astype(BF16)
            rest = (block - high.astype(F32)).astype(BF16)
            for copy in (axis, axis + 3):
                if copy < 4:
                    base = 2 * vectors * copy
                    fields[base:base + vectors, cols] = high
                    fields[base + vectors:base + 2 * vectors, cols] = rest

    chunk = 4 * HALF
    depth = 256

    def basis_chunk(step, carry):
        which = lax.rem(lax.div(r, 4) + 1 + step, n // 4)
        lanes = pl.ds(pl.multiple_of(which * chunk, chunk), chunk)
        sums = [jnp.zeros((vectors, chunk), F32) for _ in range(3)]
        for slot, (a, b) in enumerate(PAIRS):
            first_row = 2 * vectors * a
            count = 2 * vectors if a == b else 4 * vectors
            acc_high = jnp.zeros((count, chunk), F32)
            acc_rest = jnp.zeros((count, chunk), F32)
            for d in range(span // depth):
                entry = mob[slot, d * depth:(d + 1) * depth, lanes]
                high = entry.astype(BF16)
                rest = (entry - high.astype(F32)).astype(BF16)
                lhs = fields[first_row:first_row + count, d * depth:(d + 1) * depth]
                acc_high = acc_high + jnp.dot(lhs, high, preferred_element_type=F32)
                acc_rest = acc_rest + jnp.dot(lhs, rest, preferred_element_type=F32)

            def gather(base):
                return (
                    acc_high[base:base + vectors] + acc_high[base + vectors:base + 2 * vectors]
                    + acc_rest[base:base + vectors]
                )
            if a == b:
                sums[a] = sums[a] + gather(0)
            else:
                sums[b] = sums[b] + gather(0)
                sums[a] = sums[a] + gather(2 * vectors)
        for part in range(2):
            for axis in range(3):
                piece = sums[axis][:, part * LANES:(part + 1) * LANES]
                lower, upper = piece[:kh], piece[kh:]
                slot_rows = slice(kh * axis, kh * (axis + 1))
                aw_send[4 * which + 2 * part, slot_rows, :] = jnp.where(low_k, lower, swap(upper))
                aw_send[4 * which + 2 * part + 1, slot_rows, :] = jnp.where(low_k, swap(lower), upper)
        for part in range(4):
            target = 4 * which + part

            @pl.when(target != r)
            def _():
                pltpu.make_async_remote_copy(
                    src_ref=aw_send.at[target], dst_ref=aw_recv.at[r], send_sem=send_sems.at[3],
                    recv_sem=recv_sems.at[3], device_id=(target, c), device_id_type=MESH,
                ).start()
        return carry
    lax.fori_loop(0, n // 4, basis_chunk, 0)
    aw_recv[r] = aw_send[r]
    arrived(aw_recv, 3)
    aw[...] = total(aw_recv)

    rhs = [geo_ref[4 + axis:5 + axis, :] for axis in range(3)]
    row32 = lax.broadcasted_iota(jnp.int32, (vectors, LANES), 0)
    lane32 = lax.broadcasted_iota(jnp.int32, (vectors, LANES), 1)

    def unpacked(ref, axis):
        block = ref[kh * axis:kh * (axis + 1), :]
        return jnp.where(lane32 < HALF, jnp.concatenate([block, swap(block)], axis=0), 0.0)

    gram = None
    load = None
    for axis in range(3):
        w_axis = unpacked(wp_ref, axis)
        term = lax.dot_general(
            w_axis, unpacked(aw, axis), (((1,), (1,)), ((), ())),
            precision=lax.Precision.HIGHEST, preferred_element_type=F32,
        )
        load_term = w_axis * rhs[axis]
        gram = term if gram is None else gram + term
        load = load_term if load is None else load + load_term
    load = jnp.sum(load, axis=1, keepdims=True)
    wide = jnp.concatenate([gram, jnp.zeros((vectors, LANES - vectors), F32)], axis=1)
    groups = vectors // 8
    packed = wide[0:8]
    load_tile = jnp.where(lane8 == 0, load[0:8], 0.0)
    for g in range(1, groups):
        packed = packed + pltpu.roll(wide[8 * g:8 * g + 8], vectors * g, 1)
        load_tile = load_tile + jnp.where(lane8 == vectors * g, load[8 * g:8 * g + 8], 0.0)
    gram_a[0:8, :] = packed
    gram_a[8:16, :] = load_tile
    to_row(lambda peer: gram_a, gram_row, 4)
    gram_row[r] = gram_a[...]
    arrived(gram_row, 4)
    gram_b[...] = total(gram_row)
    to_col(gram_b, gram_col, 5)
    gram_col[c] = gram_b[...]
    arrived(gram_col, 5)
    both = total(gram_col)
    packed, load_tile = both[0:8], both[8:16]
    pieces, load_pieces = [packed], [load_tile]
    for g in range(1, groups):
        pieces.append(pltpu.roll(packed, LANES - vectors * g, 1))
        load_pieces.append(pltpu.roll(load_tile, LANES - vectors * g, 1))
    gram = jnp.concatenate(pieces, axis=0)
    load = jnp.concatenate(load_pieces, axis=0)[:, 0:1]

    system = jnp.where(lane32 < vectors, gram, jnp.where(lane32 == row32 + vectors, 1.0, 0.0))
    system = jnp.where(lane32 == 2 * vectors, load, system)
    for j in range(vectors):
        pivot_row = system[j:j + 1, :]
        scaled_row = pivot_row / pivot_row[:, j:j + 1]
        column = system[:, j:j + 1]
        system = jnp.where(row32 == j, scaled_row, system - column * scaled_row)
    inverse = jnp.where(jnp.logical_and(lane32 >= vectors, lane32 < 2 * vectors), system, 0.0)
    coarse = system[:, 2 * vectors:2 * vectors + 1]

    def weights_of(column):
        return jnp.where(low_k, column[:kh], column[kh:])

    def combine(ref, weights):
        out = []
        for axis in range(3):
            s = jnp.sum(ref[kh * axis:kh * (axis + 1), :] * weights, axis=0, keepdims=True)
            out.append(s + swap(s))
        return out

    def solve(vector_row):
        return weights_of(jnp.sum(inverse * vector_row, axis=1, keepdims=True))

    def dots_row(field):
        s = None
        for axis in range(3):
            term = aw[kh * axis:kh * (axis + 1), :] * field[axis]
            s = term if s is None else s + term
        lower = jnp.sum(jnp.where(low_k, s, 0.0), axis=1, keepdims=True)
        upper = jnp.sum(jnp.where(low_k, 0.0, s), axis=1, keepdims=True)
        spots = jnp.where(lane_k == row_k + vectors, lower, 0.0)
        spots = spots + jnp.where(lane_k == row_k + vectors + kh, upper, 0.0)
        return jnp.sum(spots, axis=0, keepdims=True)

    def dot_local(x, y):
        s = x[0] * y[0] + x[1] * y[1] + x[2] * y[2]
        return jnp.sum(jnp.where(low1, s, 0.0), axis=1, keepdims=True)

    def stat(ref, row_value):
        ref[...] = jnp.broadcast_to(row_value, (8, LANES))

    def at_lane(index, value):
        return jnp.where(lane1 == index, value, 0.0)

    def put(ref, field):
        ref[...] = jnp.zeros((8, LANES), F32)
        for axis in range(3):
            ref[axis:axis + 1, :] = field[axis]

    def product(vec_all, send):
        spread(vec_all, 3)
        half_tiles = tiles // 2
        for part in range(2):
            def one(i, sums):
                rows = pl.ds(pl.multiple_of(i * 8, 8), 8)
                value = [src_b[axis, rows, :] for axis in range(3)]
                out = []
                for q in range(half_tiles):
                    base = (part * half_tiles + q) * LANES
                    m = [mob[slot, rows, base:base + LANES] for slot in range(6)]
                    for axis in range(3):
                        out.append(
                            sums[3 * q + axis]
                            + (m[SLOT[axis, 0]] * value[0] + m[SLOT[axis, 1]] * value[1])
                            + m[SLOT[axis, 2]] * value[2]
                        )
                return tuple(out)
            zero = jnp.zeros((8, LANES), F32)
            sums = lax.fori_loop(0, span // 8, one, (zero,) * (3 * half_tiles), unroll=2)
            for q in range(half_tiles):
                send[part * half_tiles + q] = jnp.zeros((8, LANES), F32)
                for axis in range(3):
                    send[part * half_tiles + q, axis:axis + 1, :] = jnp.sum(
                        sums[3 * q + axis], axis=0, keepdims=True
                    )

    def mine(recv):
        tile = total(recv)
        odd = lax.rem(r, 2)
        keep = jnp.where(low1, 1 - odd, odd) == 1
        out = []
        for axis in range(3):
            half = jnp.where(keep, tile[axis:axis + 1, :], 0.0)
            out.append(half + swap(half))
        return out

    weights = weights_of(coarse)
    x0 = combine(wp_ref, weights)
    image0 = combine(aw, weights)
    r0 = [rhs[axis] - image0[axis] for axis in range(3)]

    put(vec_a, r0)
    to_col(vec_a, vec_col_a, 6)
    vec_col_a[c] = vec_a[...]
    stat(stat_a, dots_row(r0) + at_lane(0, dot_local(r0, r0)))
    to_row(lambda peer: stat_a, stat_row_a, 7)
    stat_row_a[r] = stat_a[...]
    arrived(vec_col_a, 6)
    product(vec_col_a, part_a)
    to_row(lambda peer: part_a.at[lax.div(peer, 2)], part_row_a, 8)
    part_row_a[r] = part_a[lax.div(r, 2)]
    arrived(stat_row_a, 7)
    stat_b[...] = total(stat_row_a)
    to_col(stat_b, stat_col_b, 9)
    stat_col_b[c] = stat_b[...]
    arrived(stat_col_b, 9)
    sums0 = total(stat_col_b)[0:1, :]
    norm0 = sums0[:, 0:1]
    weights = solve(sums0)
    shift = combine(wp_ref, weights)
    d0 = [r0[axis] - shift[axis] for axis in range(3)]
    shift_image = combine(aw, weights)
    arrived(part_row_a, 8)
    z0 = mine(part_row_a)
    q0 = [z0[axis] - shift_image[axis] for axis in range(3)]

    put(vec_c, q0)
    to_col(vec_c, vec_col_c, 10)
    vec_col_c[c] = vec_c[...]
    stat(
        stat_c,
        dots_row(q0) + at_lane(0, dot_local(d0, q0)) + at_lane(1, dot_local(r0, q0))
        + at_lane(2, dot_local(q0, q0)),
    )
    to_row(lambda peer: stat_c, stat_row_c, 11)
    stat_row_c[r] = stat_c[...]
    arrived(vec_col_c, 10)
    product(vec_col_c, part_c)
    to_row(lambda peer: part_c.at[lax.div(peer, 2)], part_row_c, 12)
    part_row_c[r] = part_c[lax.div(r, 2)]
    arrived(stat_row_c, 11)
    stat_d[...] = total(stat_row_c)
    to_col(stat_d, stat_col_d, 13)
    stat_col_d[c] = stat_d[...]
    arrived(stat_col_d, 13)
    sums1 = total(stat_col_d)[0:1, :]
    step0 = norm0 / sums1[:, 0:1]
    norm1 = norm0 - 2.0 * step0 * sums1[:, 1:2] + step0 * step0 * sums1[:, 2:3]
    beta = norm1 / norm0
    weights = solve(sums0 - step0 * sums1)
    shift = combine(wp_ref, weights)
    shift_image = combine(aw, weights)
    x1 = [x0[axis] + step0 * d0[axis] for axis in range(3)]
    r1 = [r0[axis] - step0 * q0[axis] for axis in range(3)]
    d1 = [r1[axis] + beta * d0[axis] - shift[axis] for axis in range(3)]
    arrived(part_row_c, 12)
    y0 = mine(part_row_c)
    q1 = [
        (z0[axis] - step0 * y0[axis]) + beta * q0[axis] - shift_image[axis] for axis in range(3)
    ]

    stat(stat_e, at_lane(0, dot_local(d1, q1)))
    to_row(lambda peer: stat_e, stat_row_e, 14)
    stat_row_e[r] = stat_e[...]
    arrived(stat_row_e, 14)
    stat_f[...] = total(stat_row_e)
    to_col(stat_f, stat_col_f, 15)
    stat_col_f[c] = stat_f[...]
    arrived(stat_col_f, 15)
    step1 = norm1 / total(stat_col_f)[0:1, 0:1]
    for axis in range(3):
        sol_ref[axis:axis + 1, :] = (x1[axis] + step1 * d1[axis])[:, :HALF]
        res_ref[axis:axis + 1, :] = (r1[axis] - step1 * q1[axis])[:, :HALF]

    for tag, dst in enumerate((
        gcol, grow, wcol, aw_recv, gram_row, gram_col, vec_col_a, stat_row_a, part_row_a,
        stat_col_b, vec_col_c, stat_row_c, part_row_c, stat_col_d, stat_row_e, stat_col_f,
    )):
        departed(dst, tag)


def body(n, positions, radii, basis, rhs):
    vectors = basis.shape[0]
    kh = vectors // 2
    span = n * HALF
    once = jnp.concatenate([positions, radii[None], rhs, jnp.zeros((1, HALF), F32)], axis=0)
    geo = jnp.concatenate([once, once], axis=1)
    wp = basis.reshape(2, kh, 3, HALF).transpose(2, 1, 0, 3).reshape(3 * kh, LANES)
    tile = pltpu.VMEM((8, LANES), F32)
    slots = pltpu.VMEM((n, 8, LANES), F32)
    parts = pltpu.VMEM((span // LANES, 8, LANES), F32)
    field_slots = pltpu.VMEM((n, 3 * kh, LANES), F32)
    two = pltpu.VMEM((16, LANES), F32)
    two_slots = pltpu.VMEM((n, 16, LANES), F32)
    vmem = pl.BlockSpec(memory_space=pltpu.VMEM)
    return pl.pallas_call(
        functools.partial(kernel, n, vectors),
        out_shape=(jax.ShapeDtypeStruct((3, HALF), F32), jax.ShapeDtypeStruct((3, HALF), F32)),
        in_specs=[vmem, vmem],
        out_specs=(vmem, vmem),
        scratch_shapes=[
            slots, slots, field_slots,
            pltpu.VMEM((4, span, LANES), F32),
            pltpu.VMEM((8, span), F32),
            pltpu.VMEM((6, span, span), F32),
            pltpu.VMEM((8 * vectors, span), BF16),
            field_slots, field_slots,
            pltpu.VMEM((3 * kh, LANES), F32),
            two, two_slots, two, two_slots,
            tile, slots, tile, slots, parts, slots, tile, slots,
            tile, slots, tile, slots, parts, slots, tile, slots,
            tile, slots, tile, slots,
            pltpu.SemaphoreType.DMA((16,)),
            pltpu.SemaphoreType.DMA((16,)),
        ],
        compiler_params=pltpu.CompilerParams(
            collective_id=0, has_side_effects=True, vmem_limit_bytes=56 << 20
        ),
    )(geo, wp)


def solution(mesh):
    return jax.shard_map(
        functools.partial(body, mesh.shape["row"]),
        mesh=mesh,
        in_specs=(
            P(None, ("row", "col")),
            P(("row", "col")),
            P(None, None, ("row", "col")),
            P(None, ("row", "col")),
        ),
        out_specs=(P(None, ("row", "col")), P(None, ("row", "col"))),
        check_vma=False,
    )
```

time: 1160 us -> 98.9 us (0.09)
  blocking collectives: 595 us -> 0 us
  matrix products: 281 us -> 0 us
  waiting for transfers between devices: 226 us -> 0 us
  Pallas kernels: 0 us -> 93.2 us
  between operations: 19.2 us -> 0.67 us
  local copies, waits for them, and re-layouts: 21.8 us -> 4.12 us
  other arithmetic: 13.2 us -> 0.67 us
    psum x5 -> x0, blocking collectives: 379 us -> none  [the longest x3 224 us: residual_stats(): lax.psum((correlation_of(field), jnp.sum(field * field)), ('row', 'col'))]
    dot_general x440 -> x0, matrix products: 280 us -> none  [the longest x432 278 us: contract(): lax.dot_general(left, right, (((1,), (1,)), ((), ())), precision=highest,...]
    unnamed x6 -> x0, waiting for transfers between devices: 226 us -> none
    all_gather x5 -> x0, blocking collectives: 152 us -> none  [the longest x3 97.6 us: body(): lax.all_gather(a, 'col', axis=2, tiled=True)]
    pallas_call x0 -> x1, Pallas kernels: none -> 93.2 us  [body(): pl.pallas_call(functools.partial(kernel, n, vectors), out_shape=(jax.Shap...]
    unnamed x2 -> x0, blocking collectives: 63.6 us -> none
    unnamed x27 -> x12, local copies, waits for them, and re-layouts: 15.4 us -> 2.59 us
  transfers between devices with their start and end apart: 3 -> 0, of which waited for: 3 -> 0; matrix products, arithmetic and copies ran while one was open for 0% -> 0% of each run, Pallas kernels for 0% -> 0%
where the time goes in v1:
time: 98.9 us; the launch traced here: 98.7 us
  Pallas kernels  93.2 us (94%)
  local copies, waits for them, and re-layouts  4.12 us (4%)
    pallas_call x1, Pallas kernels, body(): pl.pallas_call(functools.partial(kernel, n, vectors), out_shape=(jax.Shap...  93.2 us
    unnamed x12, local copies, waits for them, and re-layouts  2.59 us

profile of v1, /device:TPU:1, one launch (start us, length us, event | category | flops | bytes accessed | tf_op | source)
XLA Modules:
  0.0 98.7 jit_solution(12505295994771995087)
XLA Ops:
  0.6 0.8 copy.8
  1.5 0.0 copy-start.3
  1.5 0.7 reshape.11.wp_ref
  2.2 0.0 copy-start.2
  2.2 0.0 copy-start.4
  2.2 0.0 copy-done.3
  2.2 0.7 copy-done.2
  2.9 0.0 copy-done.4
  2.9 0.7 maximum_maximum_fusion.geo_ref
  3.5 93.2 %shard_map.59 = (f32[3,64]{1,0:T(4,128)}, f32[3,64]{1,0:T(4,128)}) custom-call(f32[8,128]{1,0:T(8,128)} %maximum_maximum_fusion.geo_ref, f32[48,128]{1,0:T(8,128)} %reshape.11.wp_ref), custom_call_target="tpu_custom_call" | custom-call | tf_op jit(solution)/shard_map/pallas_call | solution.py:453
  96.7 0.0 copy-start.1
  96.7 0.7 copy-done.1
  97.4 0.0 copy-start
  97.4 0.6 copy.11
  98.0 0.1 copy-done
  98.1 0.6 copy.12
  (1 shorter events, 0.0 us)
Async XLA Ops:
  1.5 0.7 copy-start.3
  2.2 0.7 copy-start.2
  2.2 0.7 copy-start.4
  96.7 0.7 copy-start.1
  97.4 0.7 copy-start

commit v2 on v1

--- a/solution.py
+++ b/solution.py
@@ -26,26 +26,68 @@
 
 def kernel(
     n, vectors,
-    geo_ref, wp_ref,
-    sol_ref, res_ref,
-    grow, gcol, wcol, src_b, tgt, mob, fields, aw_send, aw_recv, aw,
+    pos_ref, rad_ref, basis_ref, rhs_ref,
+    out_ref,
+    pos_in, rad_in, basis_in, rhs_in, geo, wp,
+    grow, gcol, wcol, wrow, src_b, tgt, mob, fields, w_tgt, p_tgt, aw_send, aw_recv, aw,
     gram_a, gram_row, gram_b, gram_col,
     vec_a, vec_col_a, stat_a, stat_row_a, part_a, part_row_a, stat_b, stat_col_b,
-    vec_c, vec_col_c, stat_c, stat_row_c, part_c, part_row_c, stat_d, stat_col_d,
-    stat_e, stat_row_e, stat_f, stat_col_f,
-    send_sems, recv_sems,
+    vec_c, vec_col_c, vec_row_c, part_c, part_row_c, stat_d, stat_col_d,
+    stat_f, stat_col_f,
+    in_sems, send_sems, recv_sems,
 ):
-    r = lax.axis_index("row")
-    c = lax.axis_index("col")
+    at_row = lax.axis_index("row")
+    at_col = lax.axis_index("col")
+    core = lax.rem(at_row, 2)
+    y_low = lax.rem(at_col, 2)
+    r = lax.div(at_row, 2) * 2 + y_low
+    c = lax.div(at_col, 2) * 2 + core
+
+    def row_peer(index):
+        return (lax.div(index, 2) * 2 + core, lax.div(at_col, 2) * 2 + lax.rem(index, 2))
+
+    def col_peer(index):
+        return (lax.div(at_row, 2) * 2 + lax.rem(index, 2), lax.div(index, 2) * 2 + y_low)
+
     kh = vectors // 2
     span = n * HALF
     tiles = span // LANES
 
+    barrier = pltpu.get_barrier_semaphore()
+
+    def greet(step, carry):
+        pl.semaphore_signal(
+            barrier, inc=1, device_id=row_peer(lax.rem(r + step, n)), device_id_type=MESH
+        )
+        pl.semaphore_signal(
+            barrier, inc=1, device_id=col_peer(lax.rem(c + step, n)), device_id_type=MESH
+        )
+        return carry
+    lax.fori_loop(1, n, greet, 0)
+
+    reads = [
+        pltpu.make_async_copy(src, dst, in_sems.at[i])
+        for i, (src, dst) in enumerate((
+            (pos_ref, pos_in), (rad_ref, rad_in), (basis_ref, basis_in), (rhs_ref, rhs_in)
+        ))
+    ]
+    for read in reads:
+        read.start()
+    for read in reads:
+        read.wait()
+    for half in range(2):
+        lanes = slice(half * HALF, (half + 1) * HALF)
+        geo[0:3, lanes] = pos_in[...]
+        geo[3:4, lanes] = rad_in[...]
+        for axis in range(3):
+            wp[kh * axis:kh * (axis + 1), lanes] = basis_in[axis, kh * half:kh * (half + 1), :]
+
     lane1 = lax.broadcasted_iota(jnp.int32, (1, LANES), 1)
+    lane4 = lax.broadcasted_iota(jnp.int32, (4, LANES), 1)
     lane8 = lax.broadcasted_iota(jnp.int32, (8, LANES), 1)
     lane_k = lax.broadcasted_iota(jnp.int32, (kh, LANES), 1)
     row_k = lax.broadcasted_iota(jnp.int32, (kh, LANES), 0)
-    low1, low8, low_k = lane1 < HALF, lane8 < HALF, lane_k < HALF
+    low1, low4, low_k = lane1 < HALF, lane4 < HALF, lane_k < HALF
 
     def swap(x):
         return pltpu.roll(x, HALF, 1)
@@ -55,7 +97,7 @@
             peer = lax.rem(r + step, n)
             pltpu.make_async_remote_copy(
                 src_ref=src(peer), dst_ref=dst.at[r], send_sem=send_sems.at[tag],
-                recv_sem=recv_sems.at[tag], device_id=(peer, c), device_id_type=MESH,
+                recv_sem=recv_sems.at[tag], device_id=row_peer(peer), device_id_type=MESH,
             ).start()
             return carry
         lax.fori_loop(1, n, one, 0)
@@ -65,7 +107,7 @@
             peer = lax.rem(c + step, n)
             pltpu.make_async_remote_copy(
                 src_ref=src, dst_ref=dst.at[c], send_sem=send_sems.at[tag],
-                recv_sem=recv_sems.at[tag], device_id=(r, peer), device_id_type=MESH,
+                recv_sem=recv_sems.at[tag], device_id=col_peer(peer), device_id_type=MESH,
             ).start()
             return carry
         lax.fori_loop(1, n, one, 0)
@@ -84,26 +126,21 @@
             parts = [parts[i] + parts[i + 1] for i in range(0, len(parts), 2)]
         return parts[0]
 
-    barrier = pltpu.get_barrier_semaphore()
-
-    def greet(step, carry):
-        pl.semaphore_signal(barrier, inc=1, device_id=(lax.rem(r + step, n), c), device_id_type=MESH)
-        pl.semaphore_signal(barrier, inc=1, device_id=(r, lax.rem(c + step, n)), device_id_type=MESH)
-        return carry
-    lax.fori_loop(1, n, greet, 0)
     pl.semaphore_wait(barrier, 2 * (n - 1))
 
-    to_col(geo_ref, gcol, 0)
-    to_row(lambda peer: geo_ref, grow, 1)
-    to_col(wp_ref, wcol, 2)
-    gcol[c] = geo_ref[...]
-    grow[r] = geo_ref[...]
-    wcol[c] = wp_ref[...]
+    to_col(geo, gcol, 0)
+    to_row(lambda peer: geo, grow, 1)
+    to_col(wp, wcol, 2)
+    to_row(lambda peer: wp, wrow, 14)
+    gcol[c] = geo[...]
+    grow[r] = geo[...]
+    wcol[c] = wp[...]
+    wrow[r] = wp[...]
 
     def spread(ref, count):
         for p in range(tiles):
-            tile = jnp.where(low8, ref[2 * p], ref[2 * p + 1])
-            turned = tile.T
+            tile = jnp.where(low4, ref[2 * p], ref[2 * p + 1])
+            turned = jnp.concatenate([tile, tile], axis=0).T
             for axis in range(count):
                 src_b[axis, pl.ds(p * LANES, LANES), :] = jnp.broadcast_to(
                     turned[:, axis:axis + 1], (LANES, LANES)
@@ -113,7 +150,7 @@
     spread(gcol, 4)
     arrived(grow, 1)
     for q in range(tiles):
-        tgt[:, q * LANES:(q + 1) * LANES] = jnp.where(low8, grow[2 * q], grow[2 * q + 1])
+        tgt[:, q * LANES:(q + 1) * LANES] = jnp.where(low4, grow[2 * q], grow[2 * q + 1])
 
     def form_tile(q, carry):
         lanes = pl.ds(pl.multiple_of(q * LANES, LANES), LANES)
@@ -151,15 +188,18 @@
         return carry
     lax.fori_loop(0, tiles, form_tile, 0)
 
+    def unpack_pair(ref, p, axis):
+        first = ref[2 * p, kh * axis:kh * (axis + 1), :]
+        second = ref[2 * p + 1, kh * axis:kh * (axis + 1), :]
+        return jnp.concatenate(
+            [jnp.where(low_k, first, swap(second)), jnp.where(low_k, swap(first), second)], axis=0
+        )
+
     arrived(wcol, 2)
     for p in range(tiles):
         cols = slice(p * LANES, (p + 1) * LANES)
         for axis in range(3):
-            first = wcol[2 * p, kh * axis:kh * (axis + 1), :]
-            second = wcol[2 * p + 1, kh * axis:kh * (axis + 1), :]
-            block = jnp.concatenate(
-                [jnp.where(low_k, first, swap(second)), jnp.where(low_k, swap(first), second)], axis=0
-            )
+            block = unpack_pair(wcol, p, axis)
             high = block.astype(BF16)
             rest = (block - high.astype(F32)).astype(BF16)
             for copy in (axis, axis + 3):
@@ -198,6 +238,8 @@
             else:
                 sums[b] = sums[b] + gather(0)
                 sums[a] = sums[a] + gather(2 * vectors)
+        for axis in range(3):
+            p_tgt[axis, :, lanes] = sums[axis]
         for part in range(2):
             for axis in range(3):
                 piece = sums[axis][:, part * LANES:(part + 1) * LANES]
@@ -212,31 +254,30 @@
             def _():
                 pltpu.make_async_remote_copy(
                     src_ref=aw_send.at[target], dst_ref=aw_recv.at[r], send_sem=send_sems.at[3],
-                    recv_sem=recv_sems.at[3], device_id=(target, c), device_id_type=MESH,
+                    recv_sem=recv_sems.at[3], device_id=row_peer(target), device_id_type=MESH,
                 ).start()
         return carry
     lax.fori_loop(0, n // 4, basis_chunk, 0)
     aw_recv[r] = aw_send[r]
-    arrived(aw_recv, 3)
-    aw[...] = total(aw_recv)
-
-    rhs = [geo_ref[4 + axis:5 + axis, :] for axis in range(3)]
+
+    rhs = [jnp.concatenate([rhs_in[axis:axis + 1, :]] * 2, axis=1) for axis in range(3)]
     row32 = lax.broadcasted_iota(jnp.int32, (vectors, LANES), 0)
     lane32 = lax.broadcasted_iota(jnp.int32, (vectors, LANES), 1)
 
-    def unpacked(ref, axis):
-        block = ref[kh * axis:kh * (axis + 1), :]
-        return jnp.where(lane32 < HALF, jnp.concatenate([block, swap(block)], axis=0), 0.0)
-
+    arrived(wrow, 14)
+    for p in range(tiles):
+        for axis in range(3):
+            w_tgt[axis, :, p * LANES:(p + 1) * LANES] = unpack_pair(wrow, p, axis)
     gram = None
     load = None
     for axis in range(3):
-        w_axis = unpacked(wp_ref, axis)
         term = lax.dot_general(
-            w_axis, unpacked(aw, axis), (((1,), (1,)), ((), ())),
+            w_tgt[axis], p_tgt[axis], (((1,), (1,)), ((), ())),
             precision=lax.Precision.HIGHEST, preferred_element_type=F32,
         )
-        load_term = w_axis * rhs[axis]
+        block = wp[kh * axis:kh * (axis + 1), :]
+        block = jnp.where(lane32 < HALF, jnp.concatenate([block, swap(block)], axis=0), 0.0)
+        load_term = block * rhs[axis]
         gram = term if gram is None else gram + term
         load = load_term if load is None else load + load_term
     load = jnp.sum(load, axis=1, keepdims=True)
@@ -304,19 +345,20 @@
         return jnp.sum(jnp.where(low1, s, 0.0), axis=1, keepdims=True)
 
     def stat(ref, row_value):
-        ref[...] = jnp.broadcast_to(row_value, (8, LANES))
+        ref[...] = row_value
 
     def at_lane(index, value):
         return jnp.where(lane1 == index, value, 0.0)
 
-    def put(ref, field):
-        ref[...] = jnp.zeros((8, LANES), F32)
+    def put(ref, field, last):
         for axis in range(3):
             ref[axis:axis + 1, :] = field[axis]
-
-    def product(vec_all, send):
+        ref[3:4, :] = last
+
+    def product(vec_all, send, weigh):
         spread(vec_all, 3)
         half_tiles = tiles // 2
+        dots = []
         for part in range(2):
             def one(i, sums):
                 rows = pl.ds(pl.multiple_of(i * 8, 8), 8)
@@ -335,11 +377,22 @@
             zero = jnp.zeros((8, LANES), F32)
             sums = lax.fori_loop(0, span // 8, one, (zero,) * (3 * half_tiles), unroll=2)
             for q in range(half_tiles):
-                send[part * half_tiles + q] = jnp.zeros((8, LANES), F32)
                 for axis in range(3):
-                    send[part * half_tiles + q, axis:axis + 1, :] = jnp.sum(
-                        sums[3 * q + axis], axis=0, keepdims=True
-                    )
+                    value = jnp.sum(sums[3 * q + axis], axis=0, keepdims=True)
+                    send[part * half_tiles + q, axis:axis + 1, :] = value
+                    if weigh is not None:
+                        tile = part * half_tiles + q
+                        weight = jnp.where(
+                            low1, weigh[2 * tile, axis:axis + 1, :], weigh[2 * tile + 1, axis:axis + 1, :]
+                        )
+                        dots.append(value * weight)
+        last = jnp.zeros((1, LANES), F32)
+        if weigh is not None:
+            while len(dots) > 1:
+                dots = [sum(dots[i:i + 2]) for i in range(0, len(dots), 2)]
+            last = jnp.broadcast_to(jnp.sum(dots[0], axis=1, keepdims=True), (1, LANES))
+        for q in range(tiles):
+            send[q, 3:4, :] = last
 
     def mine(recv):
         tile = total(recv)
@@ -349,21 +402,23 @@
         for axis in range(3):
             half = jnp.where(keep, tile[axis:axis + 1, :], 0.0)
             out.append(half + swap(half))
-        return out
-
+        return out, tile[3:4, :]
+
+    arrived(aw_recv, 3)
+    aw[...] = total(aw_recv)
     weights = weights_of(coarse)
-    x0 = combine(wp_ref, weights)
+    x0 = combine(wp, weights)
     image0 = combine(aw, weights)
     r0 = [rhs[axis] - image0[axis] for axis in range(3)]
 
-    put(vec_a, r0)
+    put(vec_a, r0, jnp.zeros((1, LANES), F32))
     to_col(vec_a, vec_col_a, 6)
     vec_col_a[c] = vec_a[...]
     stat(stat_a, dots_row(r0) + at_lane(0, dot_local(r0, r0)))
     to_row(lambda peer: stat_a, stat_row_a, 7)
     stat_row_a[r] = stat_a[...]
     arrived(vec_col_a, 6)
-    product(vec_col_a, part_a)
+    product(vec_col_a, part_a, None)
     to_row(lambda peer: part_a.at[lax.div(peer, 2)], part_row_a, 8)
     part_row_a[r] = part_a[lax.div(r, 2)]
     arrived(stat_row_a, 7)
@@ -374,64 +429,64 @@
     sums0 = total(stat_col_b)[0:1, :]
     norm0 = sums0[:, 0:1]
     weights = solve(sums0)
-    shift = combine(wp_ref, weights)
+    shift = combine(wp, weights)
     d0 = [r0[axis] - shift[axis] for axis in range(3)]
     shift_image = combine(aw, weights)
     arrived(part_row_a, 8)
-    z0 = mine(part_row_a)
+    z0, _ = mine(part_row_a)
     q0 = [z0[axis] - shift_image[axis] for axis in range(3)]
 
-    put(vec_c, q0)
-    to_col(vec_c, vec_col_c, 10)
-    vec_col_c[c] = vec_c[...]
-    stat(
-        stat_c,
+    put(
+        vec_c, q0,
         dots_row(q0) + at_lane(0, dot_local(d0, q0)) + at_lane(1, dot_local(r0, q0))
         + at_lane(2, dot_local(q0, q0)),
     )
-    to_row(lambda peer: stat_c, stat_row_c, 11)
-    stat_row_c[r] = stat_c[...]
+    to_col(vec_c, vec_col_c, 10)
+    to_row(lambda peer: vec_c, vec_row_c, 11)
+    vec_col_c[c] = vec_c[...]
+    vec_row_c[r] = vec_c[...]
+    arrived(vec_row_c, 11)
+    stat_d[...] = total(vec_row_c)[3:4, :]
+    to_col(stat_d, stat_col_d, 13)
+    stat_col_d[c] = stat_d[...]
     arrived(vec_col_c, 10)
-    product(vec_col_c, part_c)
+    product(vec_col_c, part_c, vec_row_c)
     to_row(lambda peer: part_c.at[lax.div(peer, 2)], part_row_c, 12)
     part_row_c[r] = part_c[lax.div(r, 2)]
-    arrived(stat_row_c, 11)
-    stat_d[...] = total(stat_row_c)
-    to_col(stat_d, stat_col_d, 13)
-    stat_col_d[c] = stat_d[...]
     arrived(stat_col_d, 13)
-    sums1 = total(stat_col_d)[0:1, :]
+    sums1 = total(stat_col_d)
     step0 = norm0 / sums1[:, 0:1]
     norm1 = norm0 - 2.0 * step0 * sums1[:, 1:2] + step0 * step0 * sums1[:, 2:3]
     beta = norm1 / norm0
     weights = solve(sums0 - step0 * sums1)
-    shift = combine(wp_ref, weights)
+    shift = combine(wp, weights)
     shift_image = combine(aw, weights)
     x1 = [x0[axis] + step0 * d0[axis] for axis in range(3)]
     r1 = [r0[axis] - step0 * q0[axis] for axis in range(3)]
     d1 = [r1[axis] + beta * d0[axis] - shift[axis] for axis in range(3)]
+    inner = jnp.sum(inverse * sums1, axis=1, keepdims=True)
+    column = jnp.sum(jnp.where(lane32 == row32 + vectors, sums1, 0.0), axis=1, keepdims=True)
+    removed = jnp.sum(inner * column, axis=0, keepdims=True)
+    factor = 1.0 + beta
+    fixed = factor * factor * sums1[:, 0:1] - 2.0 * factor * step0 * sums1[:, 2:3]
     arrived(part_row_c, 12)
-    y0 = mine(part_row_c)
+    y0, block_sum = mine(part_row_c)
+    stat_f[...] = block_sum
+    to_col(stat_f, stat_col_f, 15)
+    stat_col_f[c] = stat_f[...]
     q1 = [
         (z0[axis] - step0 * y0[axis]) + beta * q0[axis] - shift_image[axis] for axis in range(3)
     ]
-
-    stat(stat_e, at_lane(0, dot_local(d1, q1)))
-    to_row(lambda peer: stat_e, stat_row_e, 14)
-    stat_row_e[r] = stat_e[...]
-    arrived(stat_row_e, 14)
-    stat_f[...] = total(stat_row_e)
-    to_col(stat_f, stat_col_f, 15)
-    stat_col_f[c] = stat_f[...]
     arrived(stat_col_f, 15)
-    step1 = norm1 / total(stat_col_f)[0:1, 0:1]
+    curvature = fixed + step0 * step0 * (total(stat_col_f)[:, 0:1] - removed)
+    step1 = norm1 / curvature
     for axis in range(3):
-        sol_ref[axis:axis + 1, :] = (x1[axis] + step1 * d1[axis])[:, :HALF]
-        res_ref[axis:axis + 1, :] = (r1[axis] - step1 * q1[axis])[:, :HALF]
+        out_ref[axis:axis + 1, :] = x1[axis] + step1 * d1[axis]
+        out_ref[4 + axis:5 + axis, :] = r1[axis] - step1 * q1[axis]
 
     for tag, dst in enumerate((
         gcol, grow, wcol, aw_recv, gram_row, gram_col, vec_col_a, stat_row_a, part_row_a,
-        stat_col_b, vec_col_c, stat_row_c, part_row_c, stat_col_d, stat_row_e, stat_col_f,
+        stat_col_b, vec_col_c, vec_row_c, part_row_c, stat_col_d, wrow, stat_col_f,
     )):
         departed(dst, tag)
 
@@ -440,40 +495,42 @@
     vectors = basis.shape[0]
     kh = vectors // 2
     span = n * HALF
-    once = jnp.concatenate([positions, radii[None], rhs, jnp.zeros((1, HALF), F32)], axis=0)
-    geo = jnp.concatenate([once, once], axis=1)
-    wp = basis.reshape(2, kh, 3, HALF).transpose(2, 1, 0, 3).reshape(3 * kh, LANES)
-    tile = pltpu.VMEM((8, LANES), F32)
-    slots = pltpu.VMEM((n, 8, LANES), F32)
-    parts = pltpu.VMEM((span // LANES, 8, LANES), F32)
-    field_slots = pltpu.VMEM((n, 3 * kh, LANES), F32)
-    two = pltpu.VMEM((16, LANES), F32)
-    two_slots = pltpu.VMEM((n, 16, LANES), F32)
+    row, rows = pltpu.VMEM((1, LANES), F32), pltpu.VMEM((n, 1, LANES), F32)
+    tile, tile_slots = pltpu.VMEM((4, LANES), F32), pltpu.VMEM((n, 4, LANES), F32)
+    parts = pltpu.VMEM((span // LANES, 4, LANES), F32)
+    field, field_slots = pltpu.VMEM((3 * kh, LANES), F32), pltpu.VMEM((n, 3 * kh, LANES), F32)
+    two, two_slots = pltpu.VMEM((16, LANES), F32), pltpu.VMEM((n, 16, LANES), F32)
     vmem = pl.BlockSpec(memory_space=pltpu.VMEM)
-    return pl.pallas_call(
+    anywhere = pl.BlockSpec(memory_space=pl.ANY)
+    out = pl.pallas_call(
         functools.partial(kernel, n, vectors),
-        out_shape=(jax.ShapeDtypeStruct((3, HALF), F32), jax.ShapeDtypeStruct((3, HALF), F32)),
-        in_specs=[vmem, vmem],
-        out_specs=(vmem, vmem),
+        out_shape=jax.ShapeDtypeStruct((8, LANES), F32),
+        in_specs=[anywhere] * 4,
+        out_specs=vmem,
         scratch_shapes=[
-            slots, slots, field_slots,
+            pltpu.VMEM((3, HALF), F32), pltpu.VMEM((1, HALF), F32),
+            pltpu.VMEM((3, vectors, HALF), F32), pltpu.VMEM((3, HALF), F32),
+            tile, field,
+            tile_slots, tile_slots, field_slots, field_slots,
             pltpu.VMEM((4, span, LANES), F32),
-            pltpu.VMEM((8, span), F32),
+            pltpu.VMEM((4, span), F32),
             pltpu.VMEM((6, span, span), F32),
             pltpu.VMEM((8 * vectors, span), BF16),
-            field_slots, field_slots,
-            pltpu.VMEM((3 * kh, LANES), F32),
+            pltpu.VMEM((3, vectors, span), F32), pltpu.VMEM((3, vectors, span), F32),
+            field_slots, field_slots, field,
             two, two_slots, two, two_slots,
-            tile, slots, tile, slots, parts, slots, tile, slots,
-            tile, slots, tile, slots, parts, slots, tile, slots,
-            tile, slots, tile, slots,
+            tile, tile_slots, row, rows, parts, tile_slots, row, rows,
+            tile, tile_slots, tile_slots, parts, tile_slots, row, rows,
+            row, rows,
+            pltpu.SemaphoreType.DMA((4,)),
             pltpu.SemaphoreType.DMA((16,)),
             pltpu.SemaphoreType.DMA((16,)),
         ],
         compiler_params=pltpu.CompilerParams(
             collective_id=0, has_side_effects=True, vmem_limit_bytes=56 << 20
         ),
-    )(geo, wp)
+    )(positions, radii[None], basis.transpose(1, 0, 2), rhs)
+    return out[0:3, :HALF], out[4:7, :HALF]
 
 
 def solution(mesh):

time: 98.9 us -> 83.7 us (0.85)
  Pallas kernels: 93.2 us -> 81.5 us
  local copies, waits for them, and re-layouts: 4.12 us -> 1.33 us
    pallas_call x1, Pallas kernels: 93.2 us -> 81.5 us  [body(): pl.pallas_call(functools.partial(kernel, n, vectors), out_shape=jax.Shape...]
    unnamed x12 -> x0, local copies, waits for them, and re-layouts: 2.59 us -> none
    reshape x2 -> x0, local copies, waits for them, and re-layouts: 1.52 us -> none  [body(): basis.reshape(2, kh, 3, HALF).transpose(2, 1, 0, 3).reshape(3 * kh, LANES)]
    slice x0 -> x1, local copies, waits for them, and re-layouts: none -> 1.33 us  [body(): return (out[0:3, :HALF], out[4:7, :HALF])]
where the time goes in v2:
time: 83.7 us; the launch traced here: 83.5 us
  Pallas kernels  81.5 us (97%)
  local copies, waits for them, and re-layouts  1.33 us (2%)
    pallas_call x1, Pallas kernels, body(): pl.pallas_call(functools.partial(kernel, n, vectors), out_shape=jax.Shape...  81.5 us

profile of v2, /device:TPU:1, one launch (start us, length us, event | category | flops | bytes accessed | tf_op | source)
XLA Modules:
  0.0 83.5 jit_solution(11493651575915392639)
XLA Ops:
  0.6 81.5 %shard_map.59 = f32[8,128]{1,0:T(8,128)} custom-call(f32[3,64]{1,0:T(4,128)} %pos_ref.1, f32[1,64]{1,0:T(1,128)} %bitcast.3, f32[3,32,64]{2,1,0:T(8,128)} %bitcast.2, f32[3,64]{1,0:T(4,128)} %rhs_ref.1), custom_call_target="tpu_custom_call" | custom-call | tf_op jit(solution)/shard_map/pallas_call | solution.py:505
  82.2 1.3 %fusion = (f32[3,64]{1,0:T(4,128)}, f32[3,64]{1,0:T(4,128)}) fusion(f32[8,128]{1,0:T(8,128)} %shard_map.59), kind=kLoop, calls=%fused_computation | loop fusion | bytes 3072 | tf_op jit(solution)/shard_map/slice | solution.py:533

commit v3 on v2

--- a/solution.py
+++ b/solution.py
@@ -34,7 +34,7 @@
     vec_a, vec_col_a, stat_a, stat_row_a, part_a, part_row_a, stat_b, stat_col_b,
     vec_c, vec_col_c, vec_row_c, part_c, part_row_c, stat_d, stat_col_d,
     stat_f, stat_col_f,
-    in_sems, send_sems, recv_sems,
+    in_sems, send_sems, recv_sems, chunk_sems,
 ):
     at_row = lax.axis_index("row")
     at_col = lax.axis_index("col")
@@ -112,6 +112,26 @@
             return carry
         lax.fori_loop(1, n, one, 0)
 
+    chunks = n // 4
+    order = sorted(range(chunks), key=lambda k: min(k, chunks - k))
+
+    def to_col_chunks(src, dst, tag, which):
+        def one(step, carry):
+            peer = lax.rem(c + step, n)
+            pltpu.make_async_remote_copy(
+                src_ref=src, dst_ref=dst.at[c], send_sem=send_sems.at[tag],
+                recv_sem=chunk_sems.at[which, lax.div(c, 4)], device_id=col_peer(peer),
+                device_id_type=MESH,
+            ).start()
+            return carry
+        lax.fori_loop(1, n, one, 0)
+
+    def chunk_at(dst, which, step):
+        chunk = lax.rem(lax.div(c, 4) + order[step], chunks)
+        some = dst.at[pl.ds(0, 3 if step == 0 else 4)]
+        pltpu.make_async_copy(some, some, chunk_sems.at[which, chunk]).wait()
+        return chunk
+
     def arrived(dst, tag):
         all_but_one = dst.at[pl.ds(0, n - 1)]
         pltpu.make_async_copy(all_but_one, all_but_one, recv_sems.at[tag]).wait()
@@ -130,24 +150,24 @@
 
     to_col(geo, gcol, 0)
     to_row(lambda peer: geo, grow, 1)
-    to_col(wp, wcol, 2)
+    to_col_chunks(wp, wcol, 2, 0)
     to_row(lambda peer: wp, wrow, 14)
     gcol[c] = geo[...]
     grow[r] = geo[...]
     wcol[c] = wp[...]
     wrow[r] = wp[...]
 
-    def spread(ref, count):
-        for p in range(tiles):
-            tile = jnp.where(low4, ref[2 * p], ref[2 * p + 1])
-            turned = jnp.concatenate([tile, tile], axis=0).T
-            for axis in range(count):
-                src_b[axis, pl.ds(p * LANES, LANES), :] = jnp.broadcast_to(
-                    turned[:, axis:axis + 1], (LANES, LANES)
-                )
+    def spread(ref, pair, count, place):
+        tile = jnp.where(low4, ref[2 * pair], ref[2 * pair + 1])
+        turned = jnp.concatenate([tile, tile], axis=0).T
+        for axis in range(count):
+            src_b[axis, place * LANES:(place + 1) * LANES, :] = jnp.broadcast_to(
+                turned[:, axis:axis + 1], (LANES, LANES)
+            )
 
     arrived(gcol, 0)
-    spread(gcol, 4)
+    for p in range(tiles):
+        spread(gcol, p, 4, p)
     arrived(grow, 1)
     for q in range(tiles):
         tgt[:, q * LANES:(q + 1) * LANES] = jnp.where(low4, grow[2 * q], grow[2 * q + 1])
@@ -195,86 +215,71 @@
             [jnp.where(low_k, first, swap(second)), jnp.where(low_k, swap(first), second)], axis=0
         )
 
-    arrived(wcol, 2)
+    def split(x):
+        high = x.astype(BF16)
+        return high, (x - high.astype(F32)).astype(BF16)
+
+    arrived(wrow, 14)
     for p in range(tiles):
         cols = slice(p * LANES, (p + 1) * LANES)
         for axis in range(3):
-            block = unpack_pair(wcol, p, axis)
-            high = block.astype(BF16)
-            rest = (block - high.astype(F32)).astype(BF16)
-            for copy in (axis, axis + 3):
-                if copy < 4:
-                    base = 2 * vectors * copy
-                    fields[base:base + vectors, cols] = high
-                    fields[base + vectors:base + 2 * vectors, cols] = rest
-
-    chunk = 4 * HALF
-    depth = 256
-
-    def basis_chunk(step, carry):
-        which = lax.rem(lax.div(r, 4) + 1 + step, n // 4)
-        lanes = pl.ds(pl.multiple_of(which * chunk, chunk), chunk)
-        sums = [jnp.zeros((vectors, chunk), F32) for _ in range(3)]
-        for slot, (a, b) in enumerate(PAIRS):
-            first_row = 2 * vectors * a
-            count = 2 * vectors if a == b else 4 * vectors
-            acc_high = jnp.zeros((count, chunk), F32)
-            acc_rest = jnp.zeros((count, chunk), F32)
-            for d in range(span // depth):
-                entry = mob[slot, d * depth:(d + 1) * depth, lanes]
-                high = entry.astype(BF16)
-                rest = (entry - high.astype(F32)).astype(BF16)
-                lhs = fields[first_row:first_row + count, d * depth:(d + 1) * depth]
-                acc_high = acc_high + jnp.dot(lhs, high, preferred_element_type=F32)
-                acc_rest = acc_rest + jnp.dot(lhs, rest, preferred_element_type=F32)
-
-            def gather(base):
-                return (
-                    acc_high[base:base + vectors] + acc_high[base + vectors:base + 2 * vectors]
-                    + acc_rest[base:base + vectors]
-                )
-            if a == b:
-                sums[a] = sums[a] + gather(0)
-            else:
-                sums[b] = sums[b] + gather(0)
-                sums[a] = sums[a] + gather(2 * vectors)
-        for axis in range(3):
-            p_tgt[axis, :, lanes] = sums[axis]
+            high, rest = split(unpack_pair(wrow, p, axis))
+            w_tgt[axis, 0:vectors, cols] = high
+            w_tgt[axis, vectors:2 * vectors, cols] = rest
+
+    width = 4 * HALF
+    for step in range(chunks):
+        chunk = chunk_at(wcol, 0, step)
         for part in range(2):
+            cols = slice(step * width + part * LANES, step * width + (part + 1) * LANES)
             for axis in range(3):
-                piece = sums[axis][:, part * LANES:(part + 1) * LANES]
-                lower, upper = piece[:kh], piece[kh:]
-                slot_rows = slice(kh * axis, kh * (axis + 1))
-                aw_send[4 * which + 2 * part, slot_rows, :] = jnp.where(low_k, lower, swap(upper))
-                aw_send[4 * which + 2 * part + 1, slot_rows, :] = jnp.where(low_k, swap(lower), upper)
-        for part in range(4):
-            target = 4 * which + part
-
-            @pl.when(target != r)
-            def _():
-                pltpu.make_async_remote_copy(
-                    src_ref=aw_send.at[target], dst_ref=aw_recv.at[r], send_sem=send_sems.at[3],
-                    recv_sem=recv_sems.at[3], device_id=row_peer(target), device_id_type=MESH,
-                ).start()
-        return carry
-    lax.fori_loop(0, n // 4, basis_chunk, 0)
-    aw_recv[r] = aw_send[r]
+                high, rest = split(unpack_pair(wcol, 2 * chunk + part, axis))
+                for copy in (axis, axis + 3):
+                    if copy < 4:
+                        base = 2 * vectors * copy
+                        fields[base:base + vectors, cols] = high
+                        fields[base + vectors:base + 2 * vectors, cols] = rest
+
+        def basis_chunk(t, carry, step=step, chunk=chunk):
+            lanes = pl.ds(pl.multiple_of(t * width, width), width)
+            rows = pl.ds(pl.multiple_of(chunk * width, width), width)
+            sums = [None] * 3
+
+            def add(axis, value):
+                sums[axis] = value if sums[axis] is None else sums[axis] + value
+            for slot, (a, b) in enumerate(PAIRS):
+                first_row = 2 * vectors * a
+                count = 2 * vectors if a == b else 4 * vectors
+                high, rest = split(mob[slot, rows, lanes])
+                lhs = fields[first_row:first_row + count, step * width:(step + 1) * width]
+                by_high = jnp.dot(lhs, high, preferred_element_type=F32)
+                by_rest = jnp.dot(lhs, rest, preferred_element_type=F32)
+                for base, axis in ((0, b), (2 * vectors, a))[:count // (2 * vectors)]:
+                    add(axis, by_high[base:base + vectors])
+                    add(axis, by_high[base + vectors:base + 2 * vectors])
+                    add(axis, by_rest[base:base + vectors])
+            for axis in range(3):
+                if step:
+                    p_tgt[axis, :, lanes] = p_tgt[axis, :, lanes] + sums[axis]
+                else:
+                    p_tgt[axis, :, lanes] = sums[axis]
+            return carry
+        lax.fori_loop(0, span // width, basis_chunk, 0)
 
     rhs = [jnp.concatenate([rhs_in[axis:axis + 1, :]] * 2, axis=1) for axis in range(3)]
     row32 = lax.broadcasted_iota(jnp.int32, (vectors, LANES), 0)
     lane32 = lax.broadcasted_iota(jnp.int32, (vectors, LANES), 1)
 
-    arrived(wrow, 14)
-    for p in range(tiles):
-        for axis in range(3):
-            w_tgt[axis, :, p * LANES:(p + 1) * LANES] = unpack_pair(wrow, p, axis)
     gram = None
     load = None
     for axis in range(3):
-        term = lax.dot_general(
-            w_tgt[axis], p_tgt[axis], (((1,), (1,)), ((), ())),
-            precision=lax.Precision.HIGHEST, preferred_element_type=F32,
+        high, rest = split(p_tgt[axis])
+        along_lanes = (((1,), (1,)), ((), ()))
+        by_high = lax.dot_general(w_tgt[axis], high, along_lanes, preferred_element_type=F32)
+        by_rest = lax.dot_general(
+            w_tgt[axis, 0:vectors, :], rest, along_lanes, preferred_element_type=F32
         )
+        term = by_high[0:vectors] + by_high[vectors:2 * vectors] + by_rest
         block = wp[kh * axis:kh * (axis + 1), :]
         block = jnp.where(lane32 < HALF, jnp.concatenate([block, swap(block)], axis=0), 0.0)
         load_term = block * rhs[axis]
@@ -292,6 +297,16 @@
     gram_a[8:16, :] = load_tile
     to_row(lambda peer: gram_a, gram_row, 4)
     gram_row[r] = gram_a[...]
+
+    for q in range(tiles):
+        for axis in range(3):
+            piece = p_tgt[axis, :, q * LANES:(q + 1) * LANES]
+            lower, upper = piece[:kh], piece[kh:]
+            slot_rows = slice(kh * axis, kh * (axis + 1))
+            aw_send[2 * q, slot_rows, :] = jnp.where(low_k, lower, swap(upper))
+            aw_send[2 * q + 1, slot_rows, :] = jnp.where(low_k, swap(lower), upper)
+    to_row(lambda peer: aw_send.at[peer], aw_recv, 3)
+    aw_recv[r] = aw_send[r]
     arrived(gram_row, 4)
     gram_b[...] = total(gram_row)
     to_col(gram_b, gram_col, 5)
@@ -355,37 +370,46 @@
             ref[axis:axis + 1, :] = field[axis]
         ref[3:4, :] = last
 
-    def product(vec_all, send, weigh):
-        spread(vec_all, 3)
-        half_tiles = tiles // 2
+    def product(vec_all, which, send, weigh):
+        zero = jnp.zeros((8, LANES), F32)
+        sums = [zero] * (3 * tiles)
+        half = 3 * tiles // 2
+        for step in range(chunks):
+            chunk = chunk_at(vec_all, which, step)
+            for part in range(2):
+                spread(vec_all, 2 * chunk + part, 3, 2 * step + part)
+            for part in range(2):
+                def one(i, carry, step=step, chunk=chunk, part=part):
+                    rows = pl.ds(pl.multiple_of(chunk * width + i * 8, 8), 8)
+                    at = pl.ds(pl.multiple_of(step * width + i * 8, 8), 8)
+                    value = [src_b[axis, at, :] for axis in range(3)]
+                    out = []
+                    for q in range(tiles // 2):
+                        base = (part * (tiles // 2) + q) * LANES
+                        m = [mob[slot, rows, base:base + LANES] for slot in range(6)]
+                        for axis in range(3):
+                            out.append(
+                                carry[3 * q + axis]
+                                + (m[SLOT[axis, 0]] * value[0] + m[SLOT[axis, 1]] * value[1])
+                                + m[SLOT[axis, 2]] * value[2]
+                            )
+                    return tuple(out)
+                mine_sums = tuple(sums[part * half:(part + 1) * half])
+                sums[part * half:(part + 1) * half] = lax.fori_loop(
+                    0, width // 8, one, mine_sums, unroll=2
+                )
+        if weigh is not None:
+            arrived(weigh, 11)
         dots = []
-        for part in range(2):
-            def one(i, sums):
-                rows = pl.ds(pl.multiple_of(i * 8, 8), 8)
-                value = [src_b[axis, rows, :] for axis in range(3)]
-                out = []
-                for q in range(half_tiles):
-                    base = (part * half_tiles + q) * LANES
-                    m = [mob[slot, rows, base:base + LANES] for slot in range(6)]
-                    for axis in range(3):
-                        out.append(
-                            sums[3 * q + axis]
-                            + (m[SLOT[axis, 0]] * value[0] + m[SLOT[axis, 1]] * value[1])
-                            + m[SLOT[axis, 2]] * value[2]
-                        )
-                return tuple(out)
-            zero = jnp.zeros((8, LANES), F32)
-            sums = lax.fori_loop(0, span // 8, one, (zero,) * (3 * half_tiles), unroll=2)
-            for q in range(half_tiles):
-                for axis in range(3):
-                    value = jnp.sum(sums[3 * q + axis], axis=0, keepdims=True)
-                    send[part * half_tiles + q, axis:axis + 1, :] = value
-                    if weigh is not None:
-                        tile = part * half_tiles + q
-                        weight = jnp.where(
-                            low1, weigh[2 * tile, axis:axis + 1, :], weigh[2 * tile + 1, axis:axis + 1, :]
-                        )
-                        dots.append(value * weight)
+        for q in range(tiles):
+            for axis in range(3):
+                value = jnp.sum(sums[3 * q + axis], axis=0, keepdims=True)
+                send[q, axis:axis + 1, :] = value
+                if weigh is not None:
+                    weight = jnp.where(
+                        low1, weigh[2 * q, axis:axis + 1, :], weigh[2 * q + 1, axis:axis + 1, :]
+                    )
+                    dots.append(value * weight)
         last = jnp.zeros((1, LANES), F32)
         if weigh is not None:
             while len(dots) > 1:
@@ -412,13 +436,12 @@
     r0 = [rhs[axis] - image0[axis] for axis in range(3)]
 
     put(vec_a, r0, jnp.zeros((1, LANES), F32))
-    to_col(vec_a, vec_col_a, 6)
+    to_col_chunks(vec_a, vec_col_a, 6, 1)
     vec_col_a[c] = vec_a[...]
     stat(stat_a, dots_row(r0) + at_lane(0, dot_local(r0, r0)))
     to_row(lambda peer: stat_a, stat_row_a, 7)
     stat_row_a[r] = stat_a[...]
-    arrived(vec_col_a, 6)
-    product(vec_col_a, part_a, None)
+    product(vec_col_a, 1, part_a, None)
     to_row(lambda peer: part_a.at[lax.div(peer, 2)], part_row_a, 8)
     part_row_a[r] = part_a[lax.div(r, 2)]
     arrived(stat_row_a, 7)
@@ -441,18 +464,16 @@
         dots_row(q0) + at_lane(0, dot_local(d0, q0)) + at_lane(1, dot_local(r0, q0))
         + at_lane(2, dot_local(q0, q0)),
     )
-    to_col(vec_c, vec_col_c, 10)
+    to_col_chunks(vec_c, vec_col_c, 10, 2)
     to_row(lambda peer: vec_c, vec_row_c, 11)
     vec_col_c[c] = vec_c[...]
     vec_row_c[r] = vec_c[...]
-    arrived(vec_row_c, 11)
+    product(vec_col_c, 2, part_c, vec_row_c)
+    to_row(lambda peer: part_c.at[lax.div(peer, 2)], part_row_c, 12)
+    part_row_c[r] = part_c[lax.div(r, 2)]
     stat_d[...] = total(vec_row_c)[3:4, :]
     to_col(stat_d, stat_col_d, 13)
     stat_col_d[c] = stat_d[...]
-    arrived(vec_col_c, 10)
-    product(vec_col_c, part_c, vec_row_c)
-    to_row(lambda peer: part_c.at[lax.div(peer, 2)], part_row_c, 12)
-    part_row_c[r] = part_c[lax.div(r, 2)]
     arrived(stat_col_d, 13)
     sums1 = total(stat_col_d)
     step0 = norm0 / sums1[:, 0:1]
@@ -516,7 +537,7 @@
             pltpu.VMEM((4, span), F32),
             pltpu.VMEM((6, span, span), F32),
             pltpu.VMEM((8 * vectors, span), BF16),
-            pltpu.VMEM((3, vectors, span), F32), pltpu.VMEM((3, vectors, span), F32),
+            pltpu.VMEM((3, 2 * vectors, span), BF16), pltpu.VMEM((3, vectors, span), F32),
             field_slots, field_slots, field,
             two, two_slots, two, two_slots,
             tile, tile_slots, row, rows, parts, tile_slots, row, rows,
@@ -525,6 +546,7 @@
             pltpu.SemaphoreType.DMA((4,)),
             pltpu.SemaphoreType.DMA((16,)),
             pltpu.SemaphoreType.DMA((16,)),
+            pltpu.SemaphoreType.DMA((3, n // 4)),
         ],
         compiler_params=pltpu.CompilerParams(
             collective_id=0, has_side_effects=True, vmem_limit_bytes=56 << 20

time: 83.7 us -> 83.7 us (level)
  no operation moved by 1% of the time
where the time goes in v3:
time: 83.7 us; the launch traced here: 83.5 us
  Pallas kernels  81.5 us (97%)
  local copies, waits for them, and re-layouts  1.33 us (2%)
    pallas_call x1, Pallas kernels, body(): pl.pallas_call(functools.partial(kernel, n, vectors), out_shape=jax.Shape...  81.5 us

profile of v3, /device:TPU:1, one launch (start us, length us, event | category | flops | bytes accessed | tf_op | source)
XLA Modules:
  0.0 83.5 jit_solution(5587565255886937426)
XLA Ops:
  0.6 81.5 %shard_map.59 = f32[8,128]{1,0:T(8,128)} custom-call(f32[3,64]{1,0:T(4,128)} %pos_ref.1, f32[1,64]{1,0:T(1,128)} %bitcast.3, f32[3,32,64]{2,1,0:T(8,128)} %bitcast.2, f32[3,64]{1,0:T(4,128)} %rhs_ref.1), custom_call_target="tpu_custom_call" | custom-call | tf_op jit(solution)/shard_map/pallas_call | solution.py:526
  82.1 1.3 %fusion = (f32[3,64]{1,0:T(4,128)}, f32[3,64]{1,0:T(4,128)}) fusion(f32[8,128]{1,0:T(8,128)} %shard_map.59), kind=kLoop, calls=%fused_computation | loop fusion | bytes 3072 | tf_op jit(solution)/shard_map/slice | solution.py:555

commit v4 on v3

--- a/solution.py
+++ b/solution.py
@@ -29,10 +29,10 @@
     pos_ref, rad_ref, basis_ref, rhs_ref,
     out_ref,
     pos_in, rad_in, basis_in, rhs_in, geo, wp,
-    grow, gcol, wcol, wrow, src_b, tgt, mob, fields, w_tgt, p_tgt, aw_send, aw_recv, aw,
+    grow, gcol, wcol, wrow, src_b, tgt, mob, mob_high, mob_rest, fields, w_tgt, p_tgt, aw_send, aw_recv, aw,
     gram_a, gram_row, gram_b, gram_col,
     vec_a, vec_col_a, stat_a, stat_row_a, part_a, part_row_a, stat_b, stat_col_b,
-    vec_c, vec_col_c, vec_row_c, part_c, part_row_c, stat_d, stat_col_d,
+    vec_c, vec_d, vec_col_c, vec_row_c, part_c, part_row_c, stat_d, stat_col_d,
     stat_f, stat_col_f,
     in_sems, send_sems, recv_sems, chunk_sems,
 ):
@@ -172,21 +172,25 @@
     for q in range(tiles):
         tgt[:, q * LANES:(q + 1) * LANES] = jnp.where(low4, grow[2 * q], grow[2 * q + 1])
 
+    def split(x):
+        high = x.astype(BF16)
+        return high, (x - high.astype(F32)).astype(BF16)
+
     def form_tile(q, carry):
         lanes = pl.ds(pl.multiple_of(q * LANES, LANES), LANES)
         tx, ty, tz, t_rad = [
-            jnp.broadcast_to(tgt[axis:axis + 1, lanes], (8, LANES)) for axis in range(4)
+            jnp.broadcast_to(tgt[axis:axis + 1, lanes], (16, LANES)) for axis in range(4)
         ]
         t_rad_sq = t_rad * t_rad
         own = self_scale / t_rad
-        t_rel = lane8 + (q * LANES - r * HALF)
+        t_rel = lax.broadcasted_iota(jnp.int32, (16, LANES), 1) + (q * LANES - r * HALF)
         t_key = jnp.where(jnp.logical_and(t_rel >= 0, t_rel < HALF), t_rel, -span)
-        s_rel0 = lax.broadcasted_iota(jnp.int32, (8, LANES), 0) - c * HALF
+        s_rel0 = lax.broadcasted_iota(jnp.int32, (16, LANES), 0) - c * HALF
 
         def form_row(i, inner):
-            rows = pl.ds(pl.multiple_of(i * 8, 8), 8)
+            rows = pl.ds(pl.multiple_of(i * 16, 16), 16)
             sx, sy, sz, s_rad = [src_b[axis, rows, :] for axis in range(4)]
-            s_rel = s_rel0 + i * 8
+            s_rel = s_rel0 + i * 16
             same = s_rel == t_key
             dx, dy, dz = tx - sx, ty - sy, tz - sz
             dist_sq = dx * dx + dy * dy + dz * dz
@@ -197,14 +201,15 @@
             iso = jnp.where(same, own, scaled + scaled * (ratio * (1.0 / 3.0)))
             along = (scaled - scaled * ratio) * inv_sq
             ax, ay, az = along * dx, along * dy, along * dz
-            mob[0, rows, lanes] = ax * dx + iso
-            mob[1, rows, lanes] = ay * dy + iso
-            mob[2, rows, lanes] = az * dz + iso
-            mob[3, rows, lanes] = ax * dy
-            mob[4, rows, lanes] = ay * dz
-            mob[5, rows, lanes] = az * dx
+            for slot, entry in enumerate((
+                ax * dx + iso, ay * dy + iso, az * dz + iso, ax * dy, ay * dz, az * dx
+            )):
+                mob[slot, rows, lanes] = entry
+                high, rest = split(entry)
+                mob_high[slot, rows, lanes] = high
+                mob_rest[slot, rows, lanes] = rest
             return inner
-        lax.fori_loop(0, span // 8, form_row, 0, unroll=4)
+        lax.fori_loop(0, span // 16, form_row, 0, unroll=2)
         return carry
     lax.fori_loop(0, tiles, form_tile, 0)
 
@@ -215,10 +220,6 @@
             [jnp.where(low_k, first, swap(second)), jnp.where(low_k, swap(first), second)], axis=0
         )
 
-    def split(x):
-        high = x.astype(BF16)
-        return high, (x - high.astype(F32)).astype(BF16)
-
     arrived(wrow, 14)
     for p in range(tiles):
         cols = slice(p * LANES, (p + 1) * LANES)
@@ -231,7 +232,7 @@
     for step in range(chunks):
         chunk = chunk_at(wcol, 0, step)
         for part in range(2):
-            cols = slice(step * width + part * LANES, step * width + (part + 1) * LANES)
+            cols = pl.ds(pl.multiple_of(chunk * width + part * LANES, LANES), LANES)
             for axis in range(3):
                 high, rest = split(unpack_pair(wcol, 2 * chunk + part, axis))
                 for copy in (axis, axis + 3):
@@ -240,31 +241,26 @@
                         fields[base:base + vectors, cols] = high
                         fields[base + vectors:base + 2 * vectors, cols] = rest
 
-        def basis_chunk(t, carry, step=step, chunk=chunk):
-            lanes = pl.ds(pl.multiple_of(t * width, width), width)
-            rows = pl.ds(pl.multiple_of(chunk * width, width), width)
-            sums = [None] * 3
-
-            def add(axis, value):
-                sums[axis] = value if sums[axis] is None else sums[axis] + value
-            for slot, (a, b) in enumerate(PAIRS):
-                first_row = 2 * vectors * a
-                count = 2 * vectors if a == b else 4 * vectors
-                high, rest = split(mob[slot, rows, lanes])
-                lhs = fields[first_row:first_row + count, step * width:(step + 1) * width]
-                by_high = jnp.dot(lhs, high, preferred_element_type=F32)
-                by_rest = jnp.dot(lhs, rest, preferred_element_type=F32)
-                for base, axis in ((0, b), (2 * vectors, a))[:count // (2 * vectors)]:
-                    add(axis, by_high[base:base + vectors])
-                    add(axis, by_high[base + vectors:base + 2 * vectors])
-                    add(axis, by_rest[base:base + vectors])
-            for axis in range(3):
-                if step:
-                    p_tgt[axis, :, lanes] = p_tgt[axis, :, lanes] + sums[axis]
-                else:
-                    p_tgt[axis, :, lanes] = sums[axis]
-            return carry
-        lax.fori_loop(0, span // width, basis_chunk, 0)
+    def basis_chunk(t, carry):
+        lanes = pl.ds(pl.multiple_of(t * width, width), width)
+        sums = [None] * 3
+
+        def add(axis, value):
+            sums[axis] = value if sums[axis] is None else sums[axis] + value
+        for slot, (a, b) in enumerate(PAIRS):
+            first_row = 2 * vectors * a
+            count = 2 * vectors if a == b else 4 * vectors
+            lhs = fields[first_row:first_row + count, :]
+            by_high = jnp.dot(lhs, mob_high[slot, :, lanes], preferred_element_type=F32)
+            by_rest = jnp.dot(lhs, mob_rest[slot, :, lanes], preferred_element_type=F32)
+            for base, axis in ((0, b), (2 * vectors, a))[:count // (2 * vectors)]:
+                add(axis, by_high[base:base + vectors])
+                add(axis, by_high[base + vectors:base + 2 * vectors])
+                add(axis, by_rest[base:base + vectors])
+        for axis in range(3):
+            p_tgt[axis, :, lanes] = sums[axis]
+        return carry
+    lax.fori_loop(0, span // width, basis_chunk, 0)
 
     rhs = [jnp.concatenate([rhs_in[axis:axis + 1, :]] * 2, axis=1) for axis in range(3)]
     row32 = lax.broadcasted_iota(jnp.int32, (vectors, LANES), 0)
@@ -370,12 +366,14 @@
             ref[axis:axis + 1, :] = field[axis]
         ref[3:4, :] = last
 
-    def product(vec_all, which, send, weigh):
+    def product(vec_all, which, send, weigh, forward):
         zero = jnp.zeros((8, LANES), F32)
         sums = [zero] * (3 * tiles)
         half = 3 * tiles // 2
         for step in range(chunks):
             chunk = chunk_at(vec_all, which, step)
+            if step == chunks - 1:
+                forward()
             for part in range(2):
                 spread(vec_all, 2 * chunk + part, 3, 2 * step + part)
             for part in range(2):
@@ -398,8 +396,6 @@
                 sums[part * half:(part + 1) * half] = lax.fori_loop(
                     0, width // 8, one, mine_sums, unroll=2
                 )
-        if weigh is not None:
-            arrived(weigh, 11)
         dots = []
         for q in range(tiles):
             for axis in range(3):
@@ -441,13 +437,15 @@
     stat(stat_a, dots_row(r0) + at_lane(0, dot_local(r0, r0)))
     to_row(lambda peer: stat_a, stat_row_a, 7)
     stat_row_a[r] = stat_a[...]
-    product(vec_col_a, 1, part_a, None)
+
+    def forward_a():
+        arrived(stat_row_a, 7)
+        stat_b[...] = total(stat_row_a)
+        to_col(stat_b, stat_col_b, 9)
+        stat_col_b[c] = stat_b[...]
+    product(vec_col_a, 1, part_a, None, forward_a)
     to_row(lambda peer: part_a.at[lax.div(peer, 2)], part_row_a, 8)
     part_row_a[r] = part_a[lax.div(r, 2)]
-    arrived(stat_row_a, 7)
-    stat_b[...] = total(stat_row_a)
-    to_col(stat_b, stat_col_b, 9)
-    stat_col_b[c] = stat_b[...]
     arrived(stat_col_b, 9)
     sums0 = total(stat_col_b)[0:1, :]
     norm0 = sums0[:, 0:1]
@@ -459,21 +457,25 @@
     z0, _ = mine(part_row_a)
     q0 = [z0[axis] - shift_image[axis] for axis in range(3)]
 
+    put(vec_c, q0, jnp.zeros((1, LANES), F32))
+    to_col_chunks(vec_c, vec_col_c, 10, 2)
+    vec_col_c[c] = vec_c[...]
     put(
-        vec_c, q0,
+        vec_d, q0,
         dots_row(q0) + at_lane(0, dot_local(d0, q0)) + at_lane(1, dot_local(r0, q0))
         + at_lane(2, dot_local(q0, q0)),
     )
-    to_col_chunks(vec_c, vec_col_c, 10, 2)
-    to_row(lambda peer: vec_c, vec_row_c, 11)
-    vec_col_c[c] = vec_c[...]
-    vec_row_c[r] = vec_c[...]
-    product(vec_col_c, 2, part_c, vec_row_c)
+    to_row(lambda peer: vec_d, vec_row_c, 11)
+    vec_row_c[r] = vec_d[...]
+
+    def forward_c():
+        arrived(vec_row_c, 11)
+        stat_d[...] = total(vec_row_c)[3:4, :]
+        to_col(stat_d, stat_col_d, 13)
+        stat_col_d[c] = stat_d[...]
+    product(vec_col_c, 2, part_c, vec_row_c, forward_c)
     to_row(lambda peer: part_c.at[lax.div(peer, 2)], part_row_c, 12)
     part_row_c[r] = part_c[lax.div(r, 2)]
-    stat_d[...] = total(vec_row_c)[3:4, :]
-    to_col(stat_d, stat_col_d, 13)
-    stat_col_d[c] = stat_d[...]
     arrived(stat_col_d, 13)
     sums1 = total(stat_col_d)
     step0 = norm0 / sums1[:, 0:1]
@@ -536,12 +538,13 @@
             pltpu.VMEM((4, span, LANES), F32),
             pltpu.VMEM((4, span), F32),
             pltpu.VMEM((6, span, span), F32),
+            pltpu.VMEM((6, span, span), BF16), pltpu.VMEM((6, span, span), BF16),
             pltpu.VMEM((8 * vectors, span), BF16),
             pltpu.VMEM((3, 2 * vectors, span), BF16), pltpu.VMEM((3, vectors, span), F32),
             field_slots, field_slots, field,
             two, two_slots, two, two_slots,
             tile, tile_slots, row, rows, parts, tile_slots, row, rows,
-            tile, tile_slots, tile_slots, parts, tile_slots, row, rows,
+            tile, tile, tile_slots, tile_slots, parts, tile_slots, row, rows,
             row, rows,
             pltpu.SemaphoreType.DMA((4,)),
             pltpu.SemaphoreType.DMA((16,)),
@@ -549,7 +552,7 @@
             pltpu.SemaphoreType.DMA((3, n // 4)),
         ],
         compiler_params=pltpu.CompilerParams(
-            collective_id=0, has_side_effects=True, vmem_limit_bytes=56 << 20
+            collective_id=0, has_side_effects=True, vmem_limit_bytes=60 << 20
         ),
     )(positions, radii[None], basis.transpose(1, 0, 2), rhs)
     return out[0:3, :HALF], out[4:7, :HALF]

time: 83.7 us -> 87.7 us (1.048)
  Pallas kernels: 81.5 us -> 85.6 us
    pallas_call x1, Pallas kernels: 81.5 us -> 85.6 us  [body(): pl.pallas_call(functools.partial(kernel, n, vectors), out_shape=jax.Shape...]
where the time goes in v4:
time: 87.7 us; the launch traced here: 87.5 us
  Pallas kernels  85.6 us (98%)
  local copies, waits for them, and re-layouts  1.33 us (2%)
    pallas_call x1, Pallas kernels, body(): pl.pallas_call(functools.partial(kernel, n, vectors), out_shape=jax.Shape...  85.6 us

profile of v4, /device:TPU:1, one launch (start us, length us, event | category | flops | bytes accessed | tf_op | source)
XLA Modules:
  0.0 87.5 jit_solution(12085349707129890457)
XLA Ops:
  0.6 85.6 %shard_map.59 = f32[8,128]{1,0:T(8,128)} custom-call(f32[3,64]{1,0:T(4,128)} %pos_ref.1, f32[1,64]{1,0:T(1,128)} %bitcast.3, f32[3,32,64]{2,1,0:T(8,128)} %bitcast.2, f32[3,64]{1,0:T(4,128)} %rhs_ref.1), custom_call_target="tpu_custom_call" | custom-call | tf_op jit(solution)/shard_map/pallas_call | solution.py:528
  86.2 1.3 %fusion = (f32[3,64]{1,0:T(4,128)}, f32[3,64]{1,0:T(4,128)}) fusion(f32[8,128]{1,0:T(8,128)} %shard_map.59), kind=kLoop, calls=%fused_computation | loop fusion | bytes 3072 | tf_op jit(solution)/shard_map/slice | solution.py:558

commit v5 on v4

--- a/solution.py
+++ b/solution.py
@@ -179,18 +179,18 @@
     def form_tile(q, carry):
         lanes = pl.ds(pl.multiple_of(q * LANES, LANES), LANES)
         tx, ty, tz, t_rad = [
-            jnp.broadcast_to(tgt[axis:axis + 1, lanes], (16, LANES)) for axis in range(4)
+            jnp.broadcast_to(tgt[axis:axis + 1, lanes], (8, LANES)) for axis in range(4)
         ]
         t_rad_sq = t_rad * t_rad
         own = self_scale / t_rad
-        t_rel = lax.broadcasted_iota(jnp.int32, (16, LANES), 1) + (q * LANES - r * HALF)
+        t_rel = lane8 + (q * LANES - r * HALF)
         t_key = jnp.where(jnp.logical_and(t_rel >= 0, t_rel < HALF), t_rel, -span)
-        s_rel0 = lax.broadcasted_iota(jnp.int32, (16, LANES), 0) - c * HALF
+        s_rel0 = lax.broadcasted_iota(jnp.int32, (8, LANES), 0) - c * HALF
 
         def form_row(i, inner):
-            rows = pl.ds(pl.multiple_of(i * 16, 16), 16)
+            rows = pl.ds(pl.multiple_of(i * 8, 8), 8)
             sx, sy, sz, s_rad = [src_b[axis, rows, :] for axis in range(4)]
-            s_rel = s_rel0 + i * 16
+            s_rel = s_rel0 + i * 8
             same = s_rel == t_key
             dx, dy, dz = tx - sx, ty - sy, tz - sz
             dist_sq = dx * dx + dy * dy + dz * dz
@@ -201,17 +201,25 @@
             iso = jnp.where(same, own, scaled + scaled * (ratio * (1.0 / 3.0)))
             along = (scaled - scaled * ratio) * inv_sq
             ax, ay, az = along * dx, along * dy, along * dz
-            for slot, entry in enumerate((
-                ax * dx + iso, ay * dy + iso, az * dz + iso, ax * dy, ay * dz, az * dx
-            )):
-                mob[slot, rows, lanes] = entry
-                high, rest = split(entry)
-                mob_high[slot, rows, lanes] = high
-                mob_rest[slot, rows, lanes] = rest
+            mob[0, rows, lanes] = ax * dx + iso
+            mob[1, rows, lanes] = ay * dy + iso
+            mob[2, rows, lanes] = az * dz + iso
+            mob[3, rows, lanes] = ax * dy
+            mob[4, rows, lanes] = ay * dz
+            mob[5, rows, lanes] = az * dx
             return inner
-        lax.fori_loop(0, span // 16, form_row, 0, unroll=2)
+        lax.fori_loop(0, span // 8, form_row, 0, unroll=4)
         return carry
     lax.fori_loop(0, tiles, form_tile, 0)
+
+    def split_rows(i, carry):
+        rows = pl.ds(pl.multiple_of(i * 16, 16), 16)
+        for slot in range(6):
+            high, rest = split(mob[slot, rows, :])
+            mob_high[slot, rows, :] = high
+            mob_rest[slot, rows, :] = rest
+        return carry
+    lax.fori_loop(0, span // 16, split_rows, 0)
 
     def unpack_pair(ref, p, axis):
         first = ref[2 * p, kh * axis:kh * (axis + 1), :]
@@ -319,11 +327,21 @@
 
     system = jnp.where(lane32 < vectors, gram, jnp.where(lane32 == row32 + vectors, 1.0, 0.0))
     system = jnp.where(lane32 == 2 * vectors, load, system)
-    for j in range(vectors):
-        pivot_row = system[j:j + 1, :]
-        scaled_row = pivot_row / pivot_row[:, j:j + 1]
-        column = system[:, j:j + 1]
-        system = jnp.where(row32 == j, scaled_row, system - column * scaled_row)
+    for j in range(0, vectors, 2):
+        first, second = system[j:j + 1, :], system[j + 1:j + 2, :]
+        column0, column1 = system[:, j:j + 1], system[:, j + 1:j + 2]
+        p00, p01 = first[:, j:j + 1], first[:, j + 1:j + 2]
+        p10, p11 = second[:, j:j + 1], second[:, j + 1:j + 2]
+        inverse0 = 1.0 / p00
+        ahead = p01 * inverse0
+        inverse1 = 1.0 / (p11 - p10 * ahead)
+        scaled = first * inverse0
+        new1 = (second - p10 * scaled) * inverse1
+        new0 = scaled - ahead * new1
+        system = jnp.where(
+            row32 == j, new0,
+            jnp.where(row32 == j + 1, new1, system - column0 * new0 - column1 * new1),
+        )
     inverse = jnp.where(jnp.logical_and(lane32 >= vectors, lane32 < 2 * vectors), system, 0.0)
     coarse = system[:, 2 * vectors:2 * vectors + 1]
 
@@ -372,8 +390,6 @@
         half = 3 * tiles // 2
         for step in range(chunks):
             chunk = chunk_at(vec_all, which, step)
-            if step == chunks - 1:
-                forward()
             for part in range(2):
                 spread(vec_all, 2 * chunk + part, 3, 2 * step + part)
             for part in range(2):
@@ -396,6 +412,7 @@
                 sums[part * half:(part + 1) * half] = lax.fori_loop(
                     0, width // 8, one, mine_sums, unroll=2
                 )
+        forward()
         dots = []
         for q in range(tiles):
             for axis in range(3):

time: 87.7 us -> 86.4 us (0.985)
  Pallas kernels: 85.6 us -> 84.2 us
    pallas_call x1, Pallas kernels: 85.6 us -> 84.2 us  [body(): pl.pallas_call(functools.partial(kernel, n, vectors), out_shape=jax.Shape...]
where the time goes in v5:
time: 86.4 us; the launch traced here: 86.2 us
  Pallas kernels  84.2 us (97%)
  local copies, waits for them, and re-layouts  1.33 us (2%)
    pallas_call x1, Pallas kernels, body(): pl.pallas_call(functools.partial(kernel, n, vectors), out_shape=jax.Shape...  84.2 us

profile of v5, /device:TPU:1, one launch (start us, length us, event | category | flops | bytes accessed | tf_op | source)
XLA Modules:
  0.0 86.2 jit_solution(16327778142153341893)
XLA Ops:
  0.6 84.2 %shard_map.59 = f32[8,128]{1,0:T(8,128)} custom-call(f32[3,64]{1,0:T(4,128)} %pos_ref.1, f32[1,64]{1,0:T(1,128)} %bitcast.3, f32[3,32,64]{2,1,0:T(8,128)} %bitcast.2, f32[3,64]{1,0:T(4,128)} %rhs_ref.1), custom_call_target="tpu_custom_call" | custom-call | tf_op jit(solution)/shard_map/pallas_call | solution.py:545
  84.9 1.3 %fusion = (f32[3,64]{1,0:T(4,128)}, f32[3,64]{1,0:T(4,128)}) fusion(f32[8,128]{1,0:T(8,128)} %shard_map.59), kind=kLoop, calls=%fused_computation | loop fusion | bytes 3072 | tf_op jit(solution)/shard_map/slice | solution.py:575

commit v6 on v4

--- a/solution.py
+++ b/solution.py
@@ -29,7 +29,7 @@
     pos_ref, rad_ref, basis_ref, rhs_ref,
     out_ref,
     pos_in, rad_in, basis_in, rhs_in, geo, wp,
-    grow, gcol, wcol, wrow, src_b, tgt, mob, mob_high, mob_rest, fields, w_tgt, p_tgt, aw_send, aw_recv, aw,
+    grow, gcol, wcol, wrow, src_b, tgt, mob, fields, w_tgt, p_tgt, aw_send, aw_recv, aw,
     gram_a, gram_row, gram_b, gram_col,
     vec_a, vec_col_a, stat_a, stat_row_a, part_a, part_row_a, stat_b, stat_col_b,
     vec_c, vec_d, vec_col_c, vec_row_c, part_c, part_row_c, stat_d, stat_col_d,
@@ -148,7 +148,7 @@
 
     pl.semaphore_wait(barrier, 2 * (n - 1))
 
-    to_col(geo, gcol, 0)
+    to_col_chunks(geo, gcol, 0, 3)
     to_row(lambda peer: geo, grow, 1)
     to_col_chunks(wp, wcol, 2, 0)
     to_row(lambda peer: wp, wrow, 14)
@@ -161,13 +161,14 @@
         tile = jnp.where(low4, ref[2 * pair], ref[2 * pair + 1])
         turned = jnp.concatenate([tile, tile], axis=0).T
         for axis in range(count):
-            src_b[axis, place * LANES:(place + 1) * LANES, :] = jnp.broadcast_to(
+            src_b[axis, pl.ds(pl.multiple_of(place * LANES, LANES), LANES), :] = jnp.broadcast_to(
                 turned[:, axis:axis + 1], (LANES, LANES)
             )
 
-    arrived(gcol, 0)
-    for p in range(tiles):
-        spread(gcol, p, 4, p)
+    for step in range(chunks):
+        chunk = chunk_at(gcol, 3, step)
+        for part in range(2):
+            spread(gcol, 2 * chunk + part, 4, 2 * chunk + part)
     arrived(grow, 1)
     for q in range(tiles):
         tgt[:, q * LANES:(q + 1) * LANES] = jnp.where(low4, grow[2 * q], grow[2 * q + 1])
@@ -176,42 +177,53 @@
         high = x.astype(BF16)
         return high, (x - high.astype(F32)).astype(BF16)
 
+    def target_tile(q):
+        lanes = pl.ds(pl.multiple_of(q * LANES, LANES), LANES)
+        return lanes, [
+            jnp.broadcast_to(tgt[axis:axis + 1, lanes], (8, LANES)) for axis in range(4)
+        ]
+
+    def form(rows, lanes, target, target_sq, patch):
+        sx, sy, sz, s_rad = [src_b[axis, rows, :] for axis in range(4)]
+        dx, dy, dz = target[0] - sx, target[1] - sy, target[2] - sz
+        dist_sq = dx * dx + dy * dy + dz * dz
+        if patch is not None:
+            dist_sq = jnp.where(patch, 1.0, dist_sq)
+        inv = lax.rsqrt(dist_sq)
+        inv_sq = inv * inv
+        scaled = far_scale * inv
+        sized = scaled * ((target_sq + s_rad * s_rad) * inv_sq)
+        iso = scaled + sized * (1.0 / 3.0)
+        if patch is not None:
+            iso = jnp.where(patch, self_scale / target[3], iso)
+        along = (scaled - sized) * inv_sq
+        ax, ay, az = along * dx, along * dy, along * dz
+        mob[0, rows, lanes] = ax * dx + iso
+        mob[1, rows, lanes] = ay * dy + iso
+        mob[2, rows, lanes] = az * dz + iso
+        mob[3, rows, lanes] = ax * dy
+        mob[4, rows, lanes] = ay * dz
+        mob[5, rows, lanes] = az * dx
+
     def form_tile(q, carry):
-        lanes = pl.ds(pl.multiple_of(q * LANES, LANES), LANES)
-        tx, ty, tz, t_rad = [
-            jnp.broadcast_to(tgt[axis:axis + 1, lanes], (16, LANES)) for axis in range(4)
-        ]
-        t_rad_sq = t_rad * t_rad
-        own = self_scale / t_rad
-        t_rel = lax.broadcasted_iota(jnp.int32, (16, LANES), 1) + (q * LANES - r * HALF)
-        t_key = jnp.where(jnp.logical_and(t_rel >= 0, t_rel < HALF), t_rel, -span)
-        s_rel0 = lax.broadcasted_iota(jnp.int32, (16, LANES), 0) - c * HALF
+        lanes, target = target_tile(q)
+        target_sq = target[3] * target[3]
 
         def form_row(i, inner):
-            rows = pl.ds(pl.multiple_of(i * 16, 16), 16)
-            sx, sy, sz, s_rad = [src_b[axis, rows, :] for axis in range(4)]
-            s_rel = s_rel0 + i * 16
-            same = s_rel == t_key
-            dx, dy, dz = tx - sx, ty - sy, tz - sz
-            dist_sq = dx * dx + dy * dy + dz * dz
-            inv = lax.rsqrt(jnp.where(same, 1.0, dist_sq))
-            inv_sq = inv * inv
-            ratio = (t_rad_sq + s_rad * s_rad) * inv_sq
-            scaled = far_scale * inv
-            iso = jnp.where(same, own, scaled + scaled * (ratio * (1.0 / 3.0)))
-            along = (scaled - scaled * ratio) * inv_sq
-            ax, ay, az = along * dx, along * dy, along * dz
-            for slot, entry in enumerate((
-                ax * dx + iso, ay * dy + iso, az * dz + iso, ax * dy, ay * dz, az * dx
-            )):
-                mob[slot, rows, lanes] = entry
-                high, rest = split(entry)
-                mob_high[slot, rows, lanes] = high
-                mob_rest[slot, rows, lanes] = rest
+            form(pl.ds(pl.multiple_of(i * 8, 8), 8), lanes, target, target_sq, None)
             return inner
-        lax.fori_loop(0, span // 16, form_row, 0, unroll=2)
+        lax.fori_loop(0, span // 8, form_row, 0, unroll=8)
         return carry
     lax.fori_loop(0, tiles, form_tile, 0)
+
+    lanes, target = target_tile(lax.div(r, 2))
+    at_own = lane8 - lax.rem(r, 2) * HALF
+    for i in range(HALF // 8):
+        same = lax.broadcasted_iota(jnp.int32, (8, LANES), 0) + 8 * i == at_own
+        form(
+            pl.ds(pl.multiple_of(c * HALF + 8 * i, 8), 8), lanes, target,
+            target[3] * target[3], same,
+        )
 
     def unpack_pair(ref, p, axis):
         first = ref[2 * p, kh * axis:kh * (axis + 1), :]
@@ -250,9 +262,14 @@
         for slot, (a, b) in enumerate(PAIRS):
             first_row = 2 * vectors * a
             count = 2 * vectors if a == b else 4 * vectors
-            lhs = fields[first_row:first_row + count, :]
-            by_high = jnp.dot(lhs, mob_high[slot, :, lanes], preferred_element_type=F32)
-            by_rest = jnp.dot(lhs, mob_rest[slot, :, lanes], preferred_element_type=F32)
+            by_high = by_rest = None
+            for d in range(chunks):
+                high, rest = split(mob[slot, d * width:(d + 1) * width, lanes])
+                lhs = fields[first_row:first_row + count, d * width:(d + 1) * width]
+                dot_high = jnp.dot(lhs, high, preferred_element_type=F32)
+                dot_rest = jnp.dot(lhs, rest, preferred_element_type=F32)
+                by_high = dot_high if by_high is None else by_high + dot_high
+                by_rest = dot_rest if by_rest is None else by_rest + dot_rest
             for base, axis in ((0, b), (2 * vectors, a))[:count // (2 * vectors)]:
                 add(axis, by_high[base:base + vectors])
                 add(axis, by_high[base + vectors:base + 2 * vectors])
@@ -372,8 +389,6 @@
         half = 3 * tiles // 2
         for step in range(chunks):
             chunk = chunk_at(vec_all, which, step)
-            if step == chunks - 1:
-                forward()
             for part in range(2):
                 spread(vec_all, 2 * chunk + part, 3, 2 * step + part)
             for part in range(2):
@@ -396,6 +411,7 @@
                 sums[part * half:(part + 1) * half] = lax.fori_loop(
                     0, width // 8, one, mine_sums, unroll=2
                 )
+        forward()
         dots = []
         for q in range(tiles):
             for axis in range(3):
@@ -538,7 +554,6 @@
             pltpu.VMEM((4, span, LANES), F32),
             pltpu.VMEM((4, span), F32),
             pltpu.VMEM((6, span, span), F32),
-            pltpu.VMEM((6, span, span), BF16), pltpu.VMEM((6, span, span), BF16),
             pltpu.VMEM((8 * vectors, span), BF16),
             pltpu.VMEM((3, 2 * vectors, span), BF16), pltpu.VMEM((3, vectors, span), F32),
             field_slots, field_slots, field,
@@ -549,7 +564,7 @@
             pltpu.SemaphoreType.DMA((4,)),
             pltpu.SemaphoreType.DMA((16,)),
             pltpu.SemaphoreType.DMA((16,)),
-            pltpu.SemaphoreType.DMA((3, n // 4)),
+            pltpu.SemaphoreType.DMA((4, n // 4)),
         ],
         compiler_params=pltpu.CompilerParams(
             collective_id=0, has_side_effects=True, vmem_limit_bytes=60 << 20

time: 87.7 us -> 79.4 us (0.905)
  Pallas kernels: 85.6 us -> 77.3 us
    pallas_call x1, Pallas kernels: 85.6 us -> 77.3 us  [body(): pl.pallas_call(functools.partial(kernel, n, vectors), out_shape=jax.Shape...]
where the time goes in v6:
time: 79.4 us; the launch traced here: 79.3 us
  Pallas kernels  77.3 us (97%)
  local copies, waits for them, and re-layouts  1.33 us (2%)
    pallas_call x1, Pallas kernels, body(): pl.pallas_call(functools.partial(kernel, n, vectors), out_shape=jax.Shape...  77.3 us

profile of v6, /device:TPU:1, one launch (start us, length us, event | category | flops | bytes accessed | tf_op | source)
XLA Modules:
  0.0 79.3 jit_solution(17126581261303799082)
XLA Ops:
  0.6 77.3 %shard_map.59 = f32[8,128]{1,0:T(8,128)} custom-call(f32[3,64]{1,0:T(4,128)} %pos_ref.1, f32[1,64]{1,0:T(1,128)} %bitcast.3, f32[3,32,64]{2,1,0:T(8,128)} %bitcast.2, f32[3,64]{1,0:T(4,128)} %rhs_ref.1), custom_call_target="tpu_custom_call" | custom-call | tf_op jit(solution)/shard_map/pallas_call | solution.py:544
  77.9 1.3 %fusion = (f32[3,64]{1,0:T(4,128)}, f32[3,64]{1,0:T(4,128)}) fusion(f32[8,128]{1,0:T(8,128)} %shard_map.59), kind=kLoop, calls=%fused_computation | loop fusion | bytes 3072 | tf_op jit(solution)/shard_map/slice | solution.py:573

commit v7 on v6

--- a/solution.py
+++ b/solution.py
@@ -249,9 +249,9 @@
                 high, rest = split(unpack_pair(wcol, 2 * chunk + part, axis))
                 for copy in (axis, axis + 3):
                     if copy < 4:
-                        base = 2 * vectors * copy
+                        base = vectors * copy
                         fields[base:base + vectors, cols] = high
-                        fields[base + vectors:base + 2 * vectors, cols] = rest
+                        fields[4 * vectors + base:4 * vectors + base + vectors, cols] = rest
 
     def basis_chunk(t, carry):
         lanes = pl.ds(pl.multiple_of(t * width, width), width)
@@ -260,20 +260,23 @@
         def add(axis, value):
             sums[axis] = value if sums[axis] is None else sums[axis] + value
         for slot, (a, b) in enumerate(PAIRS):
-            first_row = 2 * vectors * a
-            count = 2 * vectors if a == b else 4 * vectors
+            first = vectors * a
+            count = vectors if a == b else 2 * vectors
             by_high = by_rest = None
             for d in range(chunks):
                 high, rest = split(mob[slot, d * width:(d + 1) * width, lanes])
-                lhs = fields[first_row:first_row + count, d * width:(d + 1) * width]
-                dot_high = jnp.dot(lhs, high, preferred_element_type=F32)
-                dot_rest = jnp.dot(lhs, rest, preferred_element_type=F32)
+                cols = slice(d * width, (d + 1) * width)
+                lhs_high = fields[first:first + count, cols]
+                lhs_rest = fields[4 * vectors + first:4 * vectors + first + count, cols]
+                both = jnp.concatenate([lhs_high, lhs_rest], axis=0)
+                dot_high = jnp.dot(both, high, preferred_element_type=F32)
+                dot_rest = jnp.dot(lhs_high, rest, preferred_element_type=F32)
                 by_high = dot_high if by_high is None else by_high + dot_high
                 by_rest = dot_rest if by_rest is None else by_rest + dot_rest
-            for base, axis in ((0, b), (2 * vectors, a))[:count // (2 * vectors)]:
-                add(axis, by_high[base:base + vectors])
-                add(axis, by_high[base + vectors:base + 2 * vectors])
-                add(axis, by_rest[base:base + vectors])
+            value = by_high[0:count] + by_high[count:2 * count] + by_rest
+            add(b, value[0:vectors])
+            if a != b:
+                add(a, value[vectors:2 * vectors])
         for axis in range(3):
             p_tgt[axis, :, lanes] = sums[axis]
         return carry
@@ -302,12 +305,10 @@
     wide = jnp.concatenate([gram, jnp.zeros((vectors, LANES - vectors), F32)], axis=1)
     groups = vectors // 8
     packed = wide[0:8]
-    load_tile = jnp.where(lane8 == 0, load[0:8], 0.0)
     for g in range(1, groups):
         packed = packed + pltpu.roll(wide[8 * g:8 * g + 8], vectors * g, 1)
-        load_tile = load_tile + jnp.where(lane8 == vectors * g, load[8 * g:8 * g + 8], 0.0)
     gram_a[0:8, :] = packed
-    gram_a[8:16, :] = load_tile
+    gram_a[8:9, :] = jnp.sum(jnp.where(lane32 == row32, load, 0.0), axis=0, keepdims=True)
     to_row(lambda peer: gram_a, gram_row, 4)
     gram_row[r] = gram_a[...]
 
@@ -326,13 +327,12 @@
     gram_col[c] = gram_b[...]
     arrived(gram_col, 5)
     both = total(gram_col)
-    packed, load_tile = both[0:8], both[8:16]
-    pieces, load_pieces = [packed], [load_tile]
+    packed, load_row = both[0:8], both[8:9]
+    pieces = [packed]
     for g in range(1, groups):
         pieces.append(pltpu.roll(packed, LANES - vectors * g, 1))
-        load_pieces.append(pltpu.roll(load_tile, LANES - vectors * g, 1))
     gram = jnp.concatenate(pieces, axis=0)
-    load = jnp.concatenate(load_pieces, axis=0)[:, 0:1]
+    load = jnp.sum(jnp.where(lane32 == row32, load_row, 0.0), axis=1, keepdims=True)
 
     system = jnp.where(lane32 < vectors, gram, jnp.where(lane32 == row32 + vectors, 1.0, 0.0))
     system = jnp.where(lane32 == 2 * vectors, load, system)
@@ -409,7 +409,7 @@
                     return tuple(out)
                 mine_sums = tuple(sums[part * half:(part + 1) * half])
                 sums[part * half:(part + 1) * half] = lax.fori_loop(
-                    0, width // 8, one, mine_sums, unroll=2
+                    0, width // 8, one, mine_sums, unroll=4
                 )
         forward()
         dots = []
@@ -538,7 +538,7 @@
     tile, tile_slots = pltpu.VMEM((4, LANES), F32), pltpu.VMEM((n, 4, LANES), F32)
     parts = pltpu.VMEM((span // LANES, 4, LANES), F32)
     field, field_slots = pltpu.VMEM((3 * kh, LANES), F32), pltpu.VMEM((n, 3 * kh, LANES), F32)
-    two, two_slots = pltpu.VMEM((16, LANES), F32), pltpu.VMEM((n, 16, LANES), F32)
+    two, two_slots = pltpu.VMEM((9, LANES), F32), pltpu.VMEM((n, 9, LANES), F32)
     vmem = pl.BlockSpec(memory_space=pltpu.VMEM)
     anywhere = pl.BlockSpec(memory_space=pl.ANY)
     out = pl.pallas_call(

time: 79.4 us -> 76.9 us (0.969)
  Pallas kernels: 77.3 us -> 74.8 us
    pallas_call x1, Pallas kernels: 77.3 us -> 74.8 us  [body(): pl.pallas_call(functools.partial(kernel, n, vectors), out_shape=jax.Shape...]
where the time goes in v7:
time: 76.9 us; the launch traced here: 76.7 us
  Pallas kernels  74.8 us (97%)
  local copies, waits for them, and re-layouts  1.33 us (2%)
    pallas_call x1, Pallas kernels, body(): pl.pallas_call(functools.partial(kernel, n, vectors), out_shape=jax.Shape...  74.8 us

profile of v7, /device:TPU:1, one launch (start us, length us, event | category | flops | bytes accessed | tf_op | source)
XLA Modules:
  0.0 76.7 jit_solution(8586916678245193158)
XLA Ops:
  0.6 74.8 %shard_map.59 = f32[8,128]{1,0:T(8,128)} custom-call(f32[3,64]{1,0:T(4,128)} %pos_ref.1, f32[1,64]{1,0:T(1,128)} %bitcast.3, f32[3,32,64]{2,1,0:T(8,128)} %bitcast.2, f32[3,64]{1,0:T(4,128)} %rhs_ref.1), custom_call_target="tpu_custom_call" | custom-call | tf_op jit(solution)/shard_map/pallas_call | solution.py:544
  75.4 1.3 %fusion = (f32[3,64]{1,0:T(4,128)}, f32[3,64]{1,0:T(4,128)}) fusion(f32[8,128]{1,0:T(8,128)} %shard_map.59), kind=kLoop, calls=%fused_computation | loop fusion | bytes 3072 | tf_op jit(solution)/shard_map/slice | solution.py:573

commit v8 on v7

--- a/solution.py
+++ b/solution.py
@@ -326,6 +326,8 @@
     to_col(gram_b, gram_col, 5)
     gram_col[c] = gram_b[...]
     arrived(gram_col, 5)
+    arrived(aw_recv, 3)
+    aw[...] = total(aw_recv)
     both = total(gram_col)
     packed, load_row = both[0:8], both[8:9]
     pieces = [packed]
@@ -337,9 +339,8 @@
     system = jnp.where(lane32 < vectors, gram, jnp.where(lane32 == row32 + vectors, 1.0, 0.0))
     system = jnp.where(lane32 == 2 * vectors, load, system)
     for j in range(vectors):
-        pivot_row = system[j:j + 1, :]
-        scaled_row = pivot_row / pivot_row[:, j:j + 1]
-        column = system[:, j:j + 1]
+        column = jnp.broadcast_to(system[:, j:j + 1], (vectors, LANES))
+        scaled_row = system[j:j + 1, :] * (1.0 / column[j:j + 1, :])
         system = jnp.where(row32 == j, scaled_row, system - column * scaled_row)
     inverse = jnp.where(jnp.logical_and(lane32 >= vectors, lane32 < 2 * vectors), system, 0.0)
     coarse = system[:, 2 * vectors:2 * vectors + 1]
@@ -440,10 +441,7 @@
             out.append(half + swap(half))
         return out, tile[3:4, :]
 
-    arrived(aw_recv, 3)
-    aw[...] = total(aw_recv)
     weights = weights_of(coarse)
-    x0 = combine(wp, weights)
     image0 = combine(aw, weights)
     r0 = [rhs[axis] - image0[axis] for axis in range(3)]
 
@@ -453,6 +451,7 @@
     stat(stat_a, dots_row(r0) + at_lane(0, dot_local(r0, r0)))
     to_row(lambda peer: stat_a, stat_row_a, 7)
     stat_row_a[r] = stat_a[...]
+    x0 = combine(wp, weights)
 
     def forward_a():
         arrived(stat_row_a, 7)
@@ -466,8 +465,6 @@
     sums0 = total(stat_col_b)[0:1, :]
     norm0 = sums0[:, 0:1]
     weights = solve(sums0)
-    shift = combine(wp, weights)
-    d0 = [r0[axis] - shift[axis] for axis in range(3)]
     shift_image = combine(aw, weights)
     arrived(part_row_a, 8)
     z0, _ = mine(part_row_a)
@@ -476,6 +473,8 @@
     put(vec_c, q0, jnp.zeros((1, LANES), F32))
     to_col_chunks(vec_c, vec_col_c, 10, 2)
     vec_col_c[c] = vec_c[...]
+    shift = combine(wp, weights)
+    d0 = [r0[axis] - shift[axis] for axis in range(3)]
     put(
         vec_d, q0,
         dots_row(q0) + at_lane(0, dot_local(d0, q0)) + at_lane(1, dot_local(r0, q0))

time: 76.9 us -> 76.9 us (level)
  no operation moved by 1% of the time
where the time goes in v8:
time: 76.9 us; the launch traced here: 76.7 us
  Pallas kernels  74.8 us (97%)
  local copies, waits for them, and re-layouts  1.33 us (2%)
    pallas_call x1, Pallas kernels, body(): pl.pallas_call(functools.partial(kernel, n, vectors), out_shape=jax.Shape...  74.8 us

profile of v8, /device:TPU:1, one launch (start us, length us, event | category | flops | bytes accessed | tf_op | source)
XLA Modules:
  0.0 76.7 jit_solution(2430562833466129512)
XLA Ops:
  0.6 74.8 %shard_map.59 = f32[8,128]{1,0:T(8,128)} custom-call(f32[3,64]{1,0:T(4,128)} %pos_ref.1, f32[1,64]{1,0:T(1,128)} %bitcast.3, f32[3,32,64]{2,1,0:T(8,128)} %bitcast.2, f32[3,64]{1,0:T(4,128)} %rhs_ref.1), custom_call_target="tpu_custom_call" | custom-call | tf_op jit(solution)/shard_map/pallas_call | solution.py:543
  75.4 1.3 %fusion = (f32[3,64]{1,0:T(4,128)}, f32[3,64]{1,0:T(4,128)}) fusion(f32[8,128]{1,0:T(8,128)} %shard_map.59), kind=kLoop, calls=%fused_computation | loop fusion | bytes 3072 | tf_op jit(solution)/shard_map/slice | solution.py:572

commit v9 on v8

--- a/solution.py
+++ b/solution.py
@@ -326,8 +326,6 @@
     to_col(gram_b, gram_col, 5)
     gram_col[c] = gram_b[...]
     arrived(gram_col, 5)
-    arrived(aw_recv, 3)
-    aw[...] = total(aw_recv)
     both = total(gram_col)
     packed, load_row = both[0:8], both[8:9]
     pieces = [packed]
@@ -410,7 +408,7 @@
                     return tuple(out)
                 mine_sums = tuple(sums[part * half:(part + 1) * half])
                 sums[part * half:(part + 1) * half] = lax.fori_loop(
-                    0, width // 8, one, mine_sums, unroll=4
+                    0, width // 8, one, mine_sums, unroll=8
                 )
         forward()
         dots = []
@@ -441,6 +439,8 @@
             out.append(half + swap(half))
         return out, tile[3:4, :]
 
+    arrived(aw_recv, 3)
+    aw[...] = total(aw_recv)
     weights = weights_of(coarse)
     image0 = combine(aw, weights)
     r0 = [rhs[axis] - image0[axis] for axis in range(3)]

time: 76.9 us -> 76.3 us (level)
  no operation moved by 1% of the time
where the time goes in v9:
time: 76.3 us; the launch traced here: 76.1 us
  Pallas kernels  74.2 us (97%)
  local copies, waits for them, and re-layouts  1.33 us (2%)
    pallas_call x1, Pallas kernels, body(): pl.pallas_call(functools.partial(kernel, n, vectors), out_shape=jax.Shape...  74.2 us

profile of v9, /device:TPU:1, one launch (start us, length us, event | category | flops | bytes accessed | tf_op | source)
XLA Modules:
  0.0 76.1 jit_solution(5044525086890950456)
XLA Ops:
  0.6 74.2 %shard_map.59 = f32[8,128]{1,0:T(8,128)} custom-call(f32[3,64]{1,0:T(4,128)} %pos_ref.1, f32[1,64]{1,0:T(1,128)} %bitcast.3, f32[3,32,64]{2,1,0:T(8,128)} %bitcast.2, f32[3,64]{1,0:T(4,128)} %rhs_ref.1), custom_call_target="tpu_custom_call" | custom-call | tf_op jit(solution)/shard_map/pallas_call | solution.py:543
  74.8 1.3 %fusion = (f32[3,64]{1,0:T(4,128)}, f32[3,64]{1,0:T(4,128)}) fusion(f32[8,128]{1,0:T(8,128)} %shard_map.59), kind=kLoop, calls=%fused_computation | loop fusion | bytes 3072 | tf_op jit(solution)/shard_map/slice | solution.py:572

commit v10 on v9

--- a/solution.py
+++ b/solution.py
@@ -212,7 +212,7 @@
         def form_row(i, inner):
             form(pl.ds(pl.multiple_of(i * 8, 8), 8), lanes, target, target_sq, None)
             return inner
-        lax.fori_loop(0, span // 8, form_row, 0, unroll=8)
+        lax.fori_loop(0, span // 8, form_row, 0, unroll=16)
         return carry
     lax.fori_loop(0, tiles, form_tile, 0)
 

time: 76.3 us -> 75.6 us (level)
  no operation moved by 1% of the time
where the time goes in v10:
time: 75.6 us; the launch traced here: 75.5 us
  Pallas kernels  73.5 us (97%)
  local copies, waits for them, and re-layouts  1.33 us (2%)
    pallas_call x1, Pallas kernels, body(): pl.pallas_call(functools.partial(kernel, n, vectors), out_shape=jax.Shape...  73.5 us

profile of v10, /device:TPU:1, one launch (start us, length us, event | category | flops | bytes accessed | tf_op | source)
XLA Modules:
  0.0 75.5 jit_solution(4245635282873551016)
XLA Ops:
  0.6 73.5 %shard_map.59 = f32[8,128]{1,0:T(8,128)} custom-call(f32[3,64]{1,0:T(4,128)} %pos_ref.1, f32[1,64]{1,0:T(1,128)} %bitcast.3, f32[3,32,64]{2,1,0:T(8,128)} %bitcast.2, f32[3,64]{1,0:T(4,128)} %rhs_ref.1), custom_call_target="tpu_custom_call" | custom-call | tf_op jit(solution)/shard_map/pallas_call | solution.py:543
  74.1 1.3 %fusion = (f32[3,64]{1,0:T(4,128)}, f32[3,64]{1,0:T(4,128)}) fusion(f32[8,128]{1,0:T(8,128)} %shard_map.59), kind=kLoop, calls=%fused_computation | loop fusion | bytes 3072 | tf_op jit(solution)/shard_map/slice | solution.py:572
